TPU v7x, 32 devices: a whole 2x2x4 slice. The times are simulated.
32 devices in a mesh: seq: 8 (over z, core), dp: 4 (over y, x).
Axes of the slice: x: 2, y: 2, z: 4, core: 2. Of those that a mesh axis runs over, the one named last changes fastest.
Arguments:
- query_proj: bfloat16 [3072, 2560], P(('dp', 'seq')), parts along dimension 0, may hold values from -4.5 to 4.5
- key_proj: bfloat16 [3072, 2560], P(('dp', 'seq')), parts along dimension 0, may hold values from -4.5 to 4.5
- value_proj: bfloat16 [3072, 2560], P(('dp', 'seq')), parts along dimension 0, may hold values from -16 to 16
- token_rows: int32 [3072], P('dp'), parts along dimension 0, may hold values from 0 to 767, as said below
- key_tiles: int32 [64, 4], P(('dp', 'seq')), parts along dimension 0, may hold values from 0 to 15, as said below
- key_count: int32 [64], P(('dp', 'seq')), parts along dimension 0, may hold values from 1 to 4
Outputs:
- attended: bfloat16 [3072, 2560], P(('dp', 'seq')), parts along dimension 0
There are 4 independent parts, one for each index of `dp`. A program takes and returns all parts, laid end to end along the dimension named above; each array names one. Nothing has to cross between parts.
Inputs may be any that keep to these rules, and one draw needn't show every extreme that they name: token_rows is a permutation; the rows of every aligned block of 96 frame-slab rows go to every aligned block of 96 tile-order rows exactly 96 // 8 times. `key_tiles`: for query tile i the entries m < key_count[i] are distinct, include i, and each lies between 2 * (i // 2 - 2) and 2 * (i // 2 + 2) + 1; later entries equal i.
All inputs are finite; a program needn't handle non-finite values.
Results may differ from a plain program's by a relative error of at most 0.0049.
Values may be sent and summed in bfloat16 or wider, within the bound.
No kernel may reach another device: no remote copies, remote signals or barrier semaphores. Data moves between devices by JAX's collectives and lax.ppermute only.
A program may use at most 64 MiB of HBM per device.

v0:
```python
import jax
import jax.numpy as jnp
from jax import lax
from jax.sharding import PartitionSpec as P

HD = 128
KMAX = 4
REACH = 2


def passed_along(value, axis, by):
    size = lax.axis_size(axis)
    pairs = [(i, i + by) for i in range(size) if 0 <= i + by < size]
    return lax.ppermute(value, axis, pairs)


def order_for(inverse, owner_dev, rows_dev):
    sources = lax.dynamic_slice_in_dim(inverse, owner_dev * rows_dev, rows_dev) // rows_dev
    keyed = sources * rows_dev + jnp.arange(rows_dev, dtype=jnp.int32)
    return jnp.argsort(keyed)


def attend_heads(query_rows, key_rows, value_rows, allowed, head_count):
    last = query_rows.ndim - 1

    def one_head(head_index):
        start = head_index * HD
        query_head = lax.dynamic_slice_in_dim(query_rows, start, HD, last)
        key_head = lax.dynamic_slice_in_dim(key_rows, start, HD, last)
        value_head = lax.dynamic_slice_in_dim(value_rows, start, HD, last)
        scores = jnp.einsum(
            "...qd,...kd->...qk", query_head, key_head, preferred_element_type=jnp.float32
        ) * HD ** (-0.5)
        scores = jnp.where(allowed, scores, -jnp.inf)
        peak = jnp.max(scores, axis=-1, keepdims=True)
        exponent = jnp.exp(scores - peak)
        weights = (exponent / jnp.sum(exponent, axis=-1, keepdims=True)).astype(jnp.bfloat16)
        mixed = jnp.einsum(
            "...qk,...kd->...qd", weights, value_head, preferred_element_type=jnp.float32
        )
        return mixed.astype(jnp.bfloat16)

    return lax.map(one_head, jnp.arange(head_count))


def shards(query_proj, key_proj, value_proj, token_rows, key_tiles, key_count):
    members = lax.axis_size("seq")
    myself = lax.axis_index("seq")
    rows_dev = query_proj.shape[0]
    feat_width = query_proj.shape[1]
    per_peer = rows_dev // members
    tile_rows = rows_dev // 2
    head_count = feat_width // HD
    inverse = jnp.argsort(token_rows)
    own_dest = lax.dynamic_slice_in_dim(token_rows, myself * rows_dev, rows_dev)
    send_order = jnp.argsort(own_dest)
    sorted_query = query_proj[send_order].reshape(members, per_peer, feat_width)
    sorted_keys = key_proj[send_order].reshape(members, per_peer, feat_width)
    sorted_values = value_proj[send_order].reshape(members, per_peer, feat_width)
    order_own = order_for(inverse, myself, rows_dev)
    placement_own = jnp.argsort(order_own)
    arrived_query, arrived_keys, arrived_values = (
        lax.all_to_all(sorted_query, "seq", split_axis=0, concat_axis=0, tiled=True),
        lax.all_to_all(sorted_keys, "seq", split_axis=0, concat_axis=0, tiled=True),
        lax.all_to_all(sorted_values, "seq", split_axis=0, concat_axis=0, tiled=True),
    )
    query_tile = arrived_query.reshape(rows_dev, feat_width)[placement_own]
    key_tile = arrived_keys.reshape(rows_dev, feat_width)[placement_own]
    value_tile = arrived_values.reshape(rows_dev, feat_width)[placement_own]
    blocks = []
    for offset in range(-REACH, REACH + 1):
        if offset == 0:
            blocks.append((key_tile, value_tile))
        else:
            blocks.append(passed_along((key_tile, value_tile), "seq", -offset))
    window_keys = jnp.concatenate([pair[0] for pair in blocks], axis=0)
    window_values = jnp.concatenate([pair[1] for pair in blocks], axis=0)
    entry_live = jnp.arange(KMAX)[None, :] < key_count[:, None]
    window_ids = (
        (myself + jnp.arange(-REACH, REACH + 1))[:, None] * 2 + jnp.arange(2)[None, :]
    ).reshape(-1)
    matches = (key_tiles[:, :, None] == window_ids[None, None, :]) & entry_live[:, :, None]
    listed = jnp.any(matches, axis=1)
    allowed = jnp.repeat(jnp.repeat(listed, tile_rows, axis=0), tile_rows, axis=1)
    mixed = attend_heads(query_tile, window_keys, window_values, allowed, head_count)
    tile_out = jnp.moveaxis(mixed, 0, -2).reshape(rows_dev, feat_width)
    back_send = tile_out[order_own].reshape(members, per_peer, feat_width)
    arrived_back = lax.all_to_all(back_send, "seq", split_axis=0, concat_axis=0, tiled=True)
    return arrived_back.reshape(rows_dev, feat_width)[jnp.argsort(send_order)]


def solution(mesh):
    return jax.shard_map(
        shards,
        mesh=mesh,
        in_specs=(
            P(("dp", "seq"), None),
            P(("dp", "seq"), None),
            P(("dp", "seq"), None),
            P("dp"),
            P(("dp", "seq"), None),
            P(("dp", "seq")),
        ),
        out_specs=P(("dp", "seq"), None),
        check_vma=False,
    )
```

profile of v0, /device:TPU:0, one launch (start us, length us, event | category | flops | bytes accessed | tf_op | source)
XLA Modules:
  0.0 226.7 jit_solution(4143252565832732605)
XLA Ops:
  0.0 5.1 %sort.77 = (s32[768]{0:T(1024)}, s32[768]{0:T(1024)S(1)}) sort(s32[768]{0:T(1024)} %param.11, s32[768]{0:T(1024)S(1)} %iota.41), dimensions={0}, to_apply=%region_1.2 | sort | flops 7680 | bytes 12288 | tf_op jit(solution)/shard_map/jit(argsort)/sort | solution.py:54
  6.0 2.5 %sort.78 = (s32[96]{0:T(128)}, s32[96]{0:T(128)S(1)}) sort(s32[96]{0:T(128)S(1)} %iota_add_fusion.1, s32[96]{0:T(128)S(1)} %iota.43), dimensions={0}, to_apply=%region_2.3 | sort | flops 672 | bytes 1536 | tf_op jit(solution)/shard_map/jit(argsort)/sort | solution.py:20
  8.5 2.5 %sort.76 = (s32[96]{0:T(128)}, s32[96]{0:T(128)S(1)}) sort(s32[96]{0:T(128)S(1)} %dynamic_slice.19, s32[96]{0:T(128)S(1)} %iota.40), dimensions={0}, to_apply=%region_0.0 | sort | flops 672 | bytes 1536 | tf_op jit(solution)/shard_map/jit(argsort)/sort | solution.py:56
  12.9 6.4 %all-to-all-start.2 = ((bf16[8,12,2560]{2,1,0:T(8,128)(2,1)}), bf16[8,12,2560]{2,1,0:T(8,128)(2,1)S(1)}, u32[]{:S(2)}, u32[]{:S(2)}) async-start(bf16[8,12,2560]{2,1,0:T(8,128)(2,1)} %reshape.86), calls=%async_computation.2 | async-start | bytes 1310720 | tf_op jit(solution)/shard_map/all_to_all | solution.py:65
  21.1 16.3 %all-to-all-done.2 = bf16[8,12,2560]{2,1,0:T(8,128)(2,1)S(1)} async-done(((bf16[8,12,2560]{2,1,0:T(8,128)(2,1)}), bf16[8,12,2560]{2,1,0:T(8,128)(2,1)S(1)}, u32[]{:S(2)}, u32[]{:S(2)}) %all-to-all-start.2) | async-done | bytes 491552 | tf_op jit(solution)/shard_map/all_to_all | solution.py:65
  37.4 3.5 %all-to-all-start.1 = ((bf16[8,12,2560]{2,1,0:T(8,128)(2,1)}), bf16[8,12,2560]{2,1,0:T(8,128)(2,1)S(1)}, u32[]{:S(2)}, u32[]{:S(2)}) async-start(bf16[8,12,2560]{2,1,0:T(8,128)(2,1)} %reshape.82), calls=%async_computation.1 | async-start | bytes 1310720 | tf_op jit(solution)/shard_map/all_to_all | solution.py:64
  40.9 2.5 %sort.79 = (s32[96]{0:T(128)}, s32[96]{0:T(128)S(1)}) sort(s32[96]{0:T(128)S(1)} %get-tuple-element.49, s32[96]{0:T(128)S(1)} %iota.44), dimensions={0}, to_apply=%region_3.4 | sort | flops 672 | bytes 1536 | tf_op jit(solution)/shard_map/jit(argsort)/sort | solution.py:61
  45.3 13.7 %all-to-all-done.1 = bf16[8,12,2560]{2,1,0:T(8,128)(2,1)S(1)} async-done(((bf16[8,12,2560]{2,1,0:T(8,128)(2,1)}), bf16[8,12,2560]{2,1,0:T(8,128)(2,1)S(1)}, u32[]{:S(2)}, u32[]{:S(2)}) %all-to-all-start.1) | async-done | bytes 491552 | tf_op jit(solution)/shard_map/all_to_all | solution.py:64
  59.0 3.5 %all-to-all-start = ((bf16[8,12,2560]{2,1,0:T(8,128)(2,1)}), bf16[8,12,2560]{2,1,0:T(8,128)(2,1)S(1)}, u32[]{:S(2)}, u32[]{:S(2)}) async-start(bf16[8,12,2560]{2,1,0:T(8,128)(2,1)} %reshape.80), calls=%async_computation | async-start | bytes 1310720 | tf_op jit(solution)/shard_map/all_to_all | solution.py:63
  63.6 4.6 %collective-permute-start.4 = (bf16[96,2560]{1,0:T(8,128)(2,1)S(1)}, bf16[96,2560]{1,0:T(8,128)(2,1)}, u32[]{:S(2)}, u32[]{:S(2)}) collective-permute-start(bf16[96,2560]{1,0:T(8,128)(2,1)S(1)} %gather_fusion.5), channel_id=1, source_target_pairs={{0,8},{4,12},{8,16},{12,20},{16,24},{20,28},{1,9},{5,13},{9,17},{1... | collective-permute-start | bytes 1474568 | tf_op jit(solution)/shard_map/ppermute | solution.py:14
  68.3 2.5 %collective-permute-start.5 = (bf16[96,2560]{1,0:T(8,128)(2,1)S(1)}, bf16[96,2560]{1,0:T(8,128)(2,1)}, u32[]{:S(2)}, u32[]{:S(2)}) collective-permute-start(bf16[96,2560]{1,0:T(8,128)(2,1)S(1)} %gather_fusion.5), channel_id=1, source_target_pairs={{0,4},{4,8},{8,12},{12,16},{16,20},{20,24},{24,28},{1,5},{5,9},{9,... | collective-permute-start | bytes 1474568 | tf_op jit(solution)/shard_map/ppermute | solution.py:14
  71.3 1.3 collective-permute-start.6
  72.6 1.3 collective-permute-start.7
  74.9 5.8 %collective-permute-start = (bf16[96,2560]{1,0:T(8,128)(2,1)S(1)}, bf16[96,2560]{1,0:T(8,128)(2,1)}, u32[]{:S(2)}, u32[]{:S(2)}) collective-permute-start(bf16[96,2560]{1,0:T(8,128)(2,1)S(1)} %gather_fusion.3), channel_id=1, source_target_pairs={{0,8},{4,12},{8,16},{12,20},{16,24},{20,28},{1,9},{5,13},{9,17},{1... | collective-permute-start | bytes 1474568 | tf_op jit(solution)/shard_map/ppermute | solution.py:14
  82.2 2.7 %collective-permute-done.4 = bf16[96,2560]{1,0:T(8,128)(2,1)} collective-permute-done((bf16[96,2560]{1,0:T(8,128)(2,1)S(1)}, bf16[96,2560]{1,0:T(8,128)(2,1)}, u32[]{:S(2)}, u32[]{:S(2)}) %collective-permute-start.4) | collective-permute-done | bytes 491552 | tf_op jit(solution)/shard_map/ppermute | solution.py:14
  84.9 1.6 collective-permute-start.1
  86.5 1.8 constant_dynamic-update-slice_fusion.9
  88.4 1.3 collective-permute-start.2
  89.6 1.9 constant_dynamic-update-slice_fusion.8
  92.3 3.1 %collective-permute-done = bf16[96,2560]{1,0:T(8,128)(2,1)} collective-permute-done((bf16[96,2560]{1,0:T(8,128)(2,1)S(1)}, bf16[96,2560]{1,0:T(8,128)(2,1)}, u32[]{:S(2)}, u32[]{:S(2)}) %collective-permute-start) | collective-permute-done | bytes 491552 | tf_op jit(solution)/shard_map/ppermute | solution.py:14
  95.5 1.3 collective-permute-start.3
  97.9 1.9 constant_dynamic-update-slice_fusion.6
  99.8 1.9 constant_dynamic-update-slice_fusion.5
  101.7 13.1 %collective-permute-done.3 = bf16[96,2560]{1,0:T(8,128)(2,1)S(1)} collective-permute-done((bf16[96,2560]{1,0:T(8,128)(2,1)S(1)}, bf16[96,2560]{1,0:T(8,128)(2,1)S(1)}, u32[]{:S(2)}, u32[]{:S(2)}) %collective-permute-start.3) | collective-permute-done | bytes 491552 | tf_op jit(solution)/shard_map/ppermute | solution.py:14
  114.8 1.4 copy-done.3
  116.3 79.9 %while.11 = (s32[]{:T(128)}, bf16[20,96,128]{2,1,0:T(8,128)(2,1)S(1)}, s32[20]{0:T(128)S(1)}, bf16[96,2560]{1,0:T(8,128)(2,1)S(1)}, bf16[480,2560]{1,0:T(8,128)(...) while((s32[]{:T(128)}, ...), condition=%wide.region_8.9_spmd.clone, body=%wide.region_5.8_spmd.clone.sunk | while | flops 23973700 | bytes 1052395 | solution.py:43
  117.7 1.2 fusion.20
  121.7 1.2 fusion.20
  198.1 8.8 %all-to-all-start.3 = ((bf16[8,12,2560]{2,1,0:T(8,128)(2,1)}), bf16[8,12,2560]{2,1,0:T(8,128)(2,1)S(1)}, u32[]{:S(2)}, u32[]{:S(2)}) async-start(bf16[8,12,2560]{2,1,0:T(8,128)(2,1)} %reshape.89), calls=%async_computation.3 | async-start | bytes 1310720 | tf_op jit(solution)/shard_map/all_to_all | solution.py:88
  206.8 2.5 %sort.80 = (s32[96]{0:T(128)}, s32[96]{0:T(128)S(1)}) sort(s32[96]{0:T(128)S(1)} %get-tuple-element.47, s32[96]{0:T(128)S(1)} %iota.46), dimensions={0}, to_apply=%region_9.10 | sort | flops 672 | bytes 1536 | tf_op jit(solution)/shard_map/jit(argsort)/sort | solution.py:89
  209.4 15.6 %all-to-all-done.3 = bf16[8,12,2560]{2,1,0:T(8,128)(2,1)S(1)} async-done(((bf16[8,12,2560]{2,1,0:T(8,128)(2,1)}), bf16[8,12,2560]{2,1,0:T(8,128)(2,1)S(1)}, u32[]{:S(2)}, u32[]{:S(2)}) %all-to-all-start.3) | async-done | bytes 491552 | tf_op jit(solution)/shard_map/all_to_all | solution.py:88
  225.1 1.6 gather_fusion.7
  (183 shorter events, 78.0 us)
Async XLA Ops:
  0.0 11.1 %copy-start = (bf16[96,2560]{1,0:T(8,128)(2,1)S(1)}, bf16[96,2560]{1,0:T(8,128)(2,1)}, u32[]{:S(2)}) copy-start(bf16[96,2560]{1,0:T(8,128)(2,1)} %param.10) | copy-start | bytes 1474564
  11.1 8.2 %copy-start.1 = (bf16[96,2560]{1,0:T(8,128)(2,1)S(1)}, bf16[96,2560]{1,0:T(8,128)(2,1)}, u32[]{:S(2)}) copy-start(bf16[96,2560]{1,0:T(8,128)(2,1)} %param.9) | copy-start | bytes 1474564
  12.9 24.5 %all-to-all-start.2 = ((bf16[8,12,2560]{2,1,0:T(8,128)(2,1)}), bf16[8,12,2560]{2,1,0:T(8,128)(2,1)S(1)}, u32[]{:S(2)}, u32[]{:S(2)}) async-start(bf16[8,12,2560]{2,1,0:T(8,128)(2,1)} %reshape.86), calls=%async_computation.2 | async-start | bytes 1310720 | tf_op jit(solution)/shard_map/all_to_all | solution.py:65
  19.3 24.2 %copy-start.2 = (bf16[96,2560]{1,0:T(8,128)(2,1)S(1)}, bf16[96,2560]{1,0:T(8,128)(2,1)}, u32[]{:S(2)}) copy-start(bf16[96,2560]{1,0:T(8,128)(2,1)} %param.8) | copy-start | bytes 1474564
  37.4 21.6 %all-to-all-start.1 = ((bf16[8,12,2560]{2,1,0:T(8,128)(2,1)}), bf16[8,12,2560]{2,1,0:T(8,128)(2,1)S(1)}, u32[]{:S(2)}, u32[]{:S(2)}) async-start(bf16[8,12,2560]{2,1,0:T(8,128)(2,1)} %reshape.82), calls=%async_computation.1 | async-start | bytes 1310720 | tf_op jit(solution)/shard_map/all_to_all | solution.py:64
  59.0 22.2 %all-to-all-start = ((bf16[8,12,2560]{2,1,0:T(8,128)(2,1)}), bf16[8,12,2560]{2,1,0:T(8,128)(2,1)S(1)}, u32[]{:S(2)}, u32[]{:S(2)}) async-start(bf16[8,12,2560]{2,1,0:T(8,128)(2,1)} %reshape.80), calls=%async_computation | async-start | bytes 1310720 | tf_op jit(solution)/shard_map/all_to_all | solution.py:63
  62.7 8.1 %copy-start.6 = (s32[2]{0:T(128)S(1)}, s32[2]{0:T(128)}, u32[]{:S(2)}) copy-start(s32[2]{0:T(128)} %param.13) | copy-start | bytes 28
  62.7 8.2 %copy-start.5 = (s32[2,4]{1,0:T(2,128)S(1)}, s32[2,4]{1,0:T(2,128)}, u32[]{:S(2)}) copy-start(s32[2,4]{1,0:T(2,128)} %param.12) | copy-start | bytes 100
  63.6 21.3 %collective-permute-start.4 = (bf16[96,2560]{1,0:T(8,128)(2,1)S(1)}, bf16[96,2560]{1,0:T(8,128)(2,1)}, u32[]{:S(2)}, u32[]{:S(2)}) collective-permute-start(bf16[96,2560]{1,0:T(8,128)(2,1)S(1)} %gather_fusion.5), channel_id=1, source_target_pairs={{0,8},{4,12},{8,16},{12,20},{16,24},{20,28},{1,9},{5,13},{9,17},{1... | collective-permute-start | bytes 1474568 | tf_op jit(solution)/shard_map/ppermute | solution.py:14
  68.3 20.1 %collective-permute-start.5 = (bf16[96,2560]{1,0:T(8,128)(2,1)S(1)}, bf16[96,2560]{1,0:T(8,128)(2,1)}, u32[]{:S(2)}, u32[]{:S(2)}) collective-permute-start(bf16[96,2560]{1,0:T(8,128)(2,1)S(1)} %gather_fusion.5), channel_id=1, source_target_pairs={{0,4},{4,8},{8,12},{12,16},{16,20},{20,24},{24,28},{1,5},{5,9},{9,... | collective-permute-start | bytes 1474568 | tf_op jit(solution)/shard_map/ppermute | solution.py:14
  71.3 26.6 %collective-permute-start.6 = (bf16[96,2560]{1,0:T(8,128)(2,1)S(1)}, bf16[96,2560]{1,0:T(8,128)(2,1)}, u32[]{:S(2)}, u32[]{:S(2)}) collective-permute-start(bf16[96,2560]{1,0:T(8,128)(2,1)S(1)} %gather_fusion.5), channel_id=1, source_target_pairs={{4,0},{8,4},{12,8},{16,12},{20,16},{24,20},{28,24},{5,1},{9,5},{13... | collective-permute-start | bytes 1474568 | tf_op jit(solution)/shard_map/ppermute | solution.py:14
  72.6 27.2 %collective-permute-start.7 = (bf16[96,2560]{1,0:T(8,128)(2,1)S(1)}, bf16[96,2560]{1,0:T(8,128)(2,1)}, u32[]{:S(2)}, u32[]{:S(2)}) collective-permute-start(bf16[96,2560]{1,0:T(8,128)(2,1)S(1)} %gather_fusion.5), channel_id=1, source_target_pairs={{8,0},{12,4},{16,8},{20,12},{24,16},{28,20},{9,1},{13,5},{17,9},{2... | collective-permute-start | bytes 1474568 | tf_op jit(solution)/shard_map/ppermute | solution.py:14
  74.9 20.6 %collective-permute-start = (bf16[96,2560]{1,0:T(8,128)(2,1)S(1)}, bf16[96,2560]{1,0:T(8,128)(2,1)}, u32[]{:S(2)}, u32[]{:S(2)}) collective-permute-start(bf16[96,2560]{1,0:T(8,128)(2,1)S(1)} %gather_fusion.3), channel_id=1, source_target_pairs={{0,8},{4,12},{8,16},{12,20},{16,24},{20,28},{1,9},{5,13},{9,17},{1... | collective-permute-start | bytes 1474568 | tf_op jit(solution)/shard_map/ppermute | solution.py:14
  84.9 12.9 %collective-permute-start.1 = (bf16[96,2560]{1,0:T(8,128)(2,1)S(1)}, bf16[96,2560]{1,0:T(8,128)(2,1)S(1)}, u32[]{:S(2)}, u32[]{:S(2)}) collective-permute-start(bf16[96,2560]{1,0:T(8,128)(2,1)S(1)} %gather_fusion.3), channel_id=1, source_target_pairs={{0,4},{4,8},{8,12},{12,16},{16,20},{20,24},{24,28},{1,5},{5,9},{9,... | collective-permute-start | bytes 1474568 | tf_op jit(solution)/shard_map/ppermute | solution.py:14
  88.4 13.3 %collective-permute-start.2 = (bf16[96,2560]{1,0:T(8,128)(2,1)S(1)}, bf16[96,2560]{1,0:T(8,128)(2,1)S(1)}, u32[]{:S(2)}, u32[]{:S(2)}) collective-permute-start(bf16[96,2560]{1,0:T(8,128)(2,1)S(1)} %gather_fusion.3), channel_id=1, source_target_pairs={{4,0},{8,4},{12,8},{16,12},{20,16},{24,20},{28,24},{5,1},{9,5},{13... | collective-permute-start | bytes 1474568 | tf_op jit(solution)/shard_map/ppermute | solution.py:14
  95.5 19.3 %collective-permute-start.3 = (bf16[96,2560]{1,0:T(8,128)(2,1)S(1)}, bf16[96,2560]{1,0:T(8,128)(2,1)S(1)}, u32[]{:S(2)}, u32[]{:S(2)}) collective-permute-start(bf16[96,2560]{1,0:T(8,128)(2,1)S(1)} %gather_fusion.3), channel_id=1, source_target_pairs={{8,0},{12,4},{16,8},{20,12},{24,16},{28,20},{9,1},{13,5},{17,9},{2... | collective-permute-start | bytes 1474568 | tf_op jit(solution)/shard_map/ppermute | solution.py:14
  97.9 18.4 %copy-start.4 = (bf16[20,96,128]{2,1,0:T(8,128)(2,1)S(1)}, bf16[20,96,128]{2,1,0:T(8,128)(2,1)}, u32[]{:S(2)}) copy-start(bf16[20,96,128]{2,1,0:T(8,128)(2,1)} %custom-call.18) | copy-start | bytes 1474564
  114.8 1.4 copy-start.3
  198.1 26.9 %all-to-all-start.3 = ((bf16[8,12,2560]{2,1,0:T(8,128)(2,1)}), bf16[8,12,2560]{2,1,0:T(8,128)(2,1)S(1)}, u32[]{:S(2)}, u32[]{:S(2)}) async-start(bf16[8,12,2560]{2,1,0:T(8,128)(2,1)} %reshape.89), calls=%async_computation.3 | async-start | bytes 1310720 | tf_op jit(solution)/shard_map/all_to_all | solution.py:88
where the time goes:
time: 229 us; the launch traced here: 227 us
  waiting for transfers between devices  65 us (28%)
  matrix products  47.2 us (21%)
  starting transfers between devices  41.8 us (18%)
  local copies, waits for them, and re-layouts  38.8 us (17%)
  other arithmetic  19.6 us (9%)
  loops' own time  14 us (6%)
    dot_general x20, matrix products, one_head(): jnp.einsum('...qd,...kd->...qk', query_head, key_head, preferred_element_...  24.2 us
    dot_general x20, matrix products, one_head(): jnp.einsum('...qk,...kd->...qd', weights, value_head, preferred_element_t...  23 us
    ppermute x8, starting transfers between devices, passed_along(): return lax.ppermute(value, axis, pairs)  19.6 us
    ppermute x8, waiting for transfers between devices, passed_along(): return lax.ppermute(value, axis, pairs)  18.9 us
    all_to_all x1, waiting for transfers between devices, shards(): lax.all_to_all(sorted_values, 'seq', split_axis=0, concat_axis=0, tiled=T...  16.3 us
    all_to_all x1, waiting for transfers between devices, shards(): lax.all_to_all(back_send, 'seq', split_axis=0, concat_axis=0, tiled=True)  15.6 us
    another operation x1, loops' own time, attend_heads(): return lax.map(one_head, jnp.arange(head_count))  14 us
    all_to_all x1, waiting for transfers between devices, shards(): lax.all_to_all(sorted_keys, 'seq', split_axis=0, concat_axis=0, tiled=True)  13.7 us
  transfers between devices with their start and end apart: 12, of which 7 were waited for; matrix products, arithmetic and copies ran while one was open for 10% of the time, Pallas kernels for 0%

commit v1 on v0

--- a/solution.py
+++ b/solution.py
@@ -1,6 +1,10 @@
+import functools
+
 import jax
 import jax.numpy as jnp
 from jax import lax
+from jax.experimental import pallas as pl
+from jax.experimental.pallas import tpu as pltpu
 from jax.sharding import PartitionSpec as P
 
 HD = 128
@@ -89,9 +93,179 @@
     return arrived_back.reshape(rows_dev, feat_width)[jnp.argsort(send_order)]
 
 
+META = 8
+MASKED = -1e30
+VMEM = pltpu.VMEM
+SMEM = pltpu.SMEM
+
+
+def whole(space=VMEM):
+    return pl.BlockSpec(memory_space=space)
+
+
+def params():
+    return pltpu.CompilerParams(vmem_limit_bytes=16 << 20)
+
+
+def pack_kv_kernel(group, heads, offs, tiles, count, key_ref, value_ref, *outs):
+    rows = key_ref.shape[0]
+    row = lax.broadcasted_iota(jnp.int32, (META, HD), 0)
+    lane = lax.broadcasted_iota(jnp.int32, (META, HD), 1)
+    listed = jnp.zeros((META, HD), jnp.bool_)
+    for t in range(tiles.shape[0]):
+        for m in range(tiles.shape[1]):
+            entry = jnp.where(m < count[t], tiles[t, m], -1)
+            listed = listed | ((row == t) & (lane == entry))
+    meta = jnp.where(listed, 1.0, 0.0).astype(jnp.bfloat16)
+    for j in range(group):
+        base = offs[j]
+        for h in range(heads):
+            cols = pl.ds(pl.multiple_of(base + h * HD, HD), HD)
+            outs[j][pl.ds(2 * h * rows, rows), :] = key_ref[:, cols]
+            outs[j][pl.ds((2 * h + 1) * rows, rows), :] = value_ref[:, cols]
+        outs[j][pl.ds(2 * heads * rows, META), :] = meta
+
+
+def pack_q_kernel(group, heads, offs, query_ref, *outs):
+    for j in range(group):
+        base = offs[j]
+        for h in range(heads):
+            cols = pl.ds(pl.multiple_of(base + h * HD, HD), HD)
+            outs[j][h] = query_ref[:, cols]
+
+
+def attend_kernel(blocks, heads, place_ref, tile_ref, query_ref, *refs):
+    kv, out_ref = refs[:blocks], refs[blocks]
+    rows = query_ref.shape[1]
+    lists = jnp.concatenate([r[pl.ds(2 * heads * rows, META), :] for r in kv], axis=0)
+    place = lax.broadcasted_iota(jnp.int32, (blocks * META, rows), 0) == place_ref[...]
+    mine = lax.dot_general(
+        jnp.where(place, 1.0, 0.0).astype(jnp.bfloat16), lists,
+        (((0,), (0,)), ((), ())), preferred_element_type=jnp.float32,
+    ).astype(jnp.bfloat16)
+    tile = lax.broadcasted_iota(jnp.int32, (HD, blocks * rows), 0) == tile_ref[...]
+    allowed = jnp.dot(
+        mine, jnp.where(tile, 1.0, 0.0).astype(jnp.bfloat16), preferred_element_type=jnp.float32
+    )
+    bias = jnp.where(allowed > 0.5, 0.0, MASKED)
+    for h in range(heads):
+        keys = jnp.concatenate([r[pl.ds(2 * h * rows, rows), :] for r in kv], axis=0)
+        values = jnp.concatenate([r[pl.ds((2 * h + 1) * rows, rows), :] for r in kv], axis=0)
+        scores = lax.dot_general(
+            query_ref[h], keys, (((1,), (1,)), ((), ())), preferred_element_type=jnp.float32
+        ) * HD ** (-0.5) + bias
+        peak = jnp.max(scores, axis=-1, keepdims=True)
+        exponent = jnp.exp(scores - peak)
+        total = jnp.sum(exponent, axis=-1, keepdims=True)
+        weights = (exponent / total).astype(jnp.bfloat16)
+        out_ref[h] = jnp.dot(weights, values, preferred_element_type=jnp.float32).astype(jnp.bfloat16)
+
+
+def unpack_kernel(group, heads, offs, *refs):
+    parts, out_ref = refs[:group], refs[group]
+    for j in range(group):
+        base = offs[j]
+        for h in range(heads):
+            cols = pl.ds(pl.multiple_of(base + h * HD, HD), HD)
+            out_ref[:, cols] = parts[j][h]
+
+
+def by_heads(query_proj, key_proj, value_proj, token_rows, key_tiles, key_count):
+    members = lax.axis_size("seq")
+    chips = members // 2
+    myself = lax.axis_index("seq")
+    chip, core = myself // 2, myself % 2
+    rows, feat = query_proj.shape
+    heads = feat // HD // chips
+    tiles_dev = key_tiles.shape[0]
+    tile_rows = rows // tiles_dev
+    bf16 = jnp.bfloat16
+
+    def shifted(value, by):
+        pairs = [(2 * c + k, 2 * ((c + by) % chips) + k) for c in range(chips) for k in range(2)]
+        return lax.ppermute(value, "seq", pairs)
+
+    def crossed(value):
+        return lax.ppermute(value, "seq", [(i, i ^ 1) for i in range(members)])
+
+    steps = list(range(chips))
+    offs = jnp.stack([((chip + d) % chips) * heads * HD for d in steps]).astype(jnp.int32)
+    kv_shape = jax.ShapeDtypeStruct((2 * heads * rows + META, HD), bf16)
+    q_shape = jax.ShapeDtypeStruct((heads, rows, HD), bf16)
+    kv_send = pl.pallas_call(
+        functools.partial(pack_kv_kernel, chips, heads),
+        out_shape=[kv_shape] * chips,
+        in_specs=[whole(SMEM)] * 3 + [whole()] * 2,
+        out_specs=[whole()] * chips,
+        compiler_params=params(),
+        name="pack_kv",
+    )(offs, key_tiles, key_count, key_proj, value_proj)
+    q_send = pl.pallas_call(
+        functools.partial(pack_q_kernel, chips, heads),
+        out_shape=[q_shape] * chips,
+        in_specs=[whole(SMEM), whole()],
+        out_specs=[whole()] * chips,
+        compiler_params=params(),
+        name="pack_q",
+    )(offs, query_proj)
+    kv_here = [kv_send[0]] + [shifted(kv_send[d], d) for d in steps[1:]]
+    q_here = [q_send[0]] + [shifted(q_send[d], d) for d in steps[1:]]
+    kv_there = [crossed(value) for value in kv_here]
+    kv = kv_here + kv_there
+
+    slab_tiles = (token_rows // tile_rows).reshape(members, rows)
+    source_chip = (chip - jnp.arange(chips)) % chips
+    source = jnp.concatenate([source_chip * 2 + core, source_chip * 2 + 1 - core])
+    block_tiles = slab_tiles[source]
+    key_tile = block_tiles.reshape(1, members * rows)
+    owner = block_tiles[:chips] // tiles_dev
+    place = ((chip - owner // 2) % chips + jnp.where(owner % 2 == core, 0, chips)) * META
+    place = place + block_tiles[:chips] % tiles_dev
+
+    attend = pl.pallas_call(
+        functools.partial(attend_kernel, members, heads),
+        out_shape=q_shape,
+        in_specs=[whole()] * (3 + members),
+        out_specs=whole(),
+        compiler_params=params(),
+        name="attend",
+        cost_estimate=pl.CostEstimate(
+            flops=4 * heads * rows * rows * members * HD,
+            bytes_accessed=4 * heads * rows * HD * (members + 1),
+            transcendentals=heads * rows * rows * members,
+        ),
+    )
+    outs = [attend(place[d : d + 1], key_tile, q_here[d], *kv) for d in steps]
+    back = [outs[0]] + [shifted(outs[d], -d) for d in steps[1:]]
+    return pl.pallas_call(
+        functools.partial(unpack_kernel, chips, heads),
+        out_shape=jax.ShapeDtypeStruct((rows, feat), bf16),
+        in_specs=[whole(SMEM)] + [whole()] * chips,
+        out_specs=whole(),
+        compiler_params=params(),
+        name="unpack",
+    )(offs, *back)
+
+
+def shards_of(*args):
+    members = lax.axis_size("seq")
+    rows, feat = args[0].shape
+    chips = members // 2
+    tiles = args[4].shape[0]
+    if (
+        members % 2 == 0
+        and feat // HD % chips == 0
+        and rows % 16 == 0
+        and tiles <= META
+        and tiles * members <= HD
+    ):
+        return by_heads(*args)
+    return shards(*args)
+
+
 def solution(mesh):
     return jax.shard_map(
-        shards,
+        shards_of,
         mesh=mesh,
         in_specs=(
             P(("dp", "seq"), None),

time: 229 us -> 59.9 us (0.26)
  waiting for transfers between devices: 65 us -> 14.5 us
  matrix products: 47.2 us -> 0 us
  local copies, waits for them, and re-layouts: 38.8 us -> 2.79 us
  other arithmetic: 19.6 us -> 0.22 us
  loops' own time: 14 us -> 0 us
  Pallas kernels: 0 us -> 12.3 us
  starting transfers between devices: 41.8 us -> 29.8 us
    dot_general x40 -> x0, matrix products: 47.2 us -> none  [the longest x20 24.2 us: one_head(): jnp.einsum('...qd,...kd->...qk', query_head, key_head, preferred_element_...]
    all_to_all x4 -> x0, waiting for transfers between devices: 46.1 us -> none  [the longest x1 16.3 us: shards(): lax.all_to_all(sorted_values, 'seq', split_axis=0, concat_axis=0, tiled=T...]
    all_to_all x4 -> x0, starting transfers between devices: 22.2 us -> none  [the longest x1 8.77 us: shards(): lax.all_to_all(back_send, 'seq', split_axis=0, concat_axis=0, tiled=True)]
    sort x5 -> x0, other arithmetic: 15.3 us -> none  [the longest x1 5.11 us: shards(): inverse = jnp.argsort(token_rows)]
    another operation x1 -> x0, loops' own time: 14 us -> none  [attend_heads(): return lax.map(one_head, jnp.arange(head_count))]
    dynamic_slice x21 -> x0, local copies, waits for them, and re-layouts: 12.5 us -> none  [the longest x20 11.7 us: attend_heads(): return lax.map(one_head, jnp.arange(head_count))]
    pallas_call x0 -> x7, Pallas kernels: none -> 12.3 us  [the longest x4 9.5 us: by_heads(): outs = [attend(place[d:d + 1], key_tile, q_here[d], *kv) for d in steps]]
    ppermute x8 -> x13, starting transfers between devices: 19.6 us -> 29.8 us  [the longest x9 29.2 us: shifted(): return lax.ppermute(value, 'seq', pairs)]
  transfers between devices with their start and end apart: 12 -> 13, of which waited for: 7 -> 3; matrix products, arithmetic and copies ran while one was open for 10% -> 1% of each run, Pallas kernels for 0% -> 17%
where the time goes in v1:
time: 59.9 us; the launch traced here: 59.7 us
  starting transfers between devices  29.8 us (50%)
  waiting for transfers between devices  14.5 us (24%)
  Pallas kernels  12.3 us (21%)
  local copies, waits for them, and re-layouts  2.79 us (5%)
    ppermute x9, starting transfers between devices, shifted(): return lax.ppermute(value, 'seq', pairs)  29.2 us
    ppermute x9, waiting for transfers between devices, shifted(): return lax.ppermute(value, 'seq', pairs)  14.5 us
    pallas_call x4, Pallas kernels, by_heads(): outs = [attend(place[d:d + 1], key_tile, q_here[d], *kv) for d in steps]  9.5 us
    unnamed x12, local copies, waits for them, and re-layouts  2.08 us
    pallas_call x1, Pallas kernels, by_heads(): pl.pallas_call(functools.partial(unpack_kernel, chips, heads), out_shape=...  1.41 us
  transfers between devices with their start and end apart: 13, of which 3 were waited for; matrix products, arithmetic and copies ran while one was open for 1% of the time, Pallas kernels for 17%

profile of v1, /device:TPU:0, one launch (start us, length us, event | category | flops | bytes accessed | tf_op | source)
XLA Modules:
  0.0 59.7 jit_solution(213734145577056434)
XLA Ops:
  0.0 0.1 pad_add_fusion.offs
  0.1 1.0 %copy-done = bf16[96,2560]{1,0:T(8,128)(2,1)S(1)} copy-done((bf16[96,2560]{1,0:T(8,128)(2,1)S(1)}, bf16[96,2560]{1,0:T(8,128)(2,1)}, u32[]{:S(2)}) %copy-start) | copy-done | bytes 491544
  1.1 0.6 %pack_q.1 = (bf16[5,96,128]{2,1,0:T(8,128)(2,1)S(1)}, bf16[5,96,128]{2,1,0:T(8,128)(2,1)S(1)}, bf16[5,96,128]{2,1,0:T(8,128)(2,1)S(1)}, bf16[5,96,128]{2,1,0:T(8,128)(2,1)S(1)}) custom-call(s32[4]{0:T(128)S(1)} %pad_add_fusion.offs, bf16[96,2560]{1,0:T(8,128)(2,1)S(1)} %copy-done), custom_call_target="tpu_custom_call" | custom-call | tf_op jit(solution)/shard_map/pack_q/pallas_call | solution.py:203
  1.8 0.0 copy-start.3
  1.8 0.0 copy-start.4
  1.8 3.1 %collective-permute-start.7 = (bf16[5,96,128]{2,1,0:T(8,128)(2,1)S(1)}, bf16[5,96,128]{2,1,0:T(8,128)(2,1)S(1)}, u32[]{:S(2)}, u32[]{:S(2)}) collective-permute-start(bf16[5,96,128]{2,1,0:T(8,128)(2,1)S(1)} %get-tuple-element.18), channel_id=1, source_target_pairs={{0,8},{4,12},{8,16},{12,20},{16,24},{20,28},{24,0},{28,4},{1,9},{5... | collective-permute-start | bytes 368648 | tf_op jit(solution)/shard_map/ppermute | solution.py:186
  4.9 1.0 %copy-done.2 = bf16[96,2560]{1,0:T(8,128)(2,1)S(1)} copy-done((bf16[96,2560]{1,0:T(8,128)(2,1)S(1)}, bf16[96,2560]{1,0:T(8,128)(2,1)}, u32[]{:S(2)}) %copy-start.2) | copy-done | bytes 491544
  5.9 0.8 %pack_kv.1 = (bf16[968,128]{1,0:T(8,128)(2,1)S(1)}, bf16[968,128]{1,0:T(8,128)(2,1)S(1)}, bf16[968,128]{1,0:T(8,128)(2,1)S(1)}, bf16[968,128]{1,0:T(8,128)(2,1)S(1)}) custom-call(s32[4]{0:T(128)S(1)} %pad_add_fusion.offs, s32[2,4]{1,0:T(2,128)S(1)} %copy-done.3, s32[2]{0:T(128)S(1)} %copy-done.4, bf16[96,2560]{1,0:T(8,128)(2,1)S(1)} %copy-done.1, ...), custom_call_target="tpu_custom_call" | custom-call | tf_op jit(solution)/shard_map/pack_kv/pallas_call | solution.py:195
  6.7 1.6 %collective-permute-start = (bf16[968,128]{1,0:T(8,128)(2,1)S(1)}, bf16[968,128]{1,0:T(8,128)(2,1)S(1)}, u32[]{:S(2)}, u32[]{:S(2)}) collective-permute-start(bf16[968,128]{1,0:T(8,128)(2,1)S(1)} %get-tuple-element.15), channel_id=1, source_target_pairs={{0,8},{4,12},{8,16},{12,20},{16,24},{20,28},{24,0},{28,4},{1,9},{5... | collective-permute-start | bytes 743432 | tf_op jit(solution)/shard_map/ppermute | solution.py:186
  8.3 1.6 %collective-permute-start.1 = (bf16[968,128]{1,0:T(8,128)(2,1)S(1)}, bf16[968,128]{1,0:T(8,128)(2,1)S(1)}, u32[]{:S(2)}, u32[]{:S(2)}) collective-permute-start(bf16[968,128]{1,0:T(8,128)(2,1)S(1)} %get-tuple-element.16), channel_id=1, source_target_pairs={{0,16},{4,20},{8,24},{12,28},{16,0},{20,4},{24,8},{28,12},{1,17},{... | collective-permute-start | bytes 743432 | tf_op jit(solution)/shard_map/ppermute | solution.py:186
  10.0 2.3 %collective-permute-start.2 = (bf16[968,128]{1,0:T(8,128)(2,1)S(1)}, bf16[968,128]{1,0:T(8,128)(2,1)S(1)}, u32[]{:S(2)}, u32[]{:S(2)}) collective-permute-start(bf16[968,128]{1,0:T(8,128)(2,1)S(1)} %get-tuple-element.17), channel_id=1, source_target_pairs={{0,24},{4,28},{8,0},{12,4},{16,8},{20,12},{24,16},{28,20},{1,25},{... | collective-permute-start | bytes 743432 | tf_op jit(solution)/shard_map/ppermute | solution.py:186
  12.3 0.1 fusion.11
  12.4 0.1 reshape.59
  12.5 0.6 gather_fusion
  13.0 4.5 %collective-permute-done.refs_1_ = bf16[968,128]{1,0:T(8,128)(2,1)S(1)} collective-permute-done((bf16[968,128]{1,0:T(8,128)(2,1)S(1)}, bf16[968,128]{1,0:T(8,128)(2,1)S(1)}, u32[]{:S(2)}, u32[]{:S(2)}) %collective-permute-start) | collective-permute-done | bytes 247840 | tf_op jit(solution)/shard_map/ppermute | solution.py:186
  17.6 9.2 %collective-permute-done.1.refs_2_ = bf16[968,128]{1,0:T(8,128)(2,1)S(1)} collective-permute-done((bf16[968,128]{1,0:T(8,128)(2,1)S(1)}, bf16[968,128]{1,0:T(8,128)(2,1)S(1)}, u32[]{:S(2)}, u32[]{:S(2)}) %collective-permute-start.1) | collective-permute-done | bytes 247840 | tf_op jit(solution)/shard_map/ppermute | solution.py:186
  26.8 0.5 collective-permute-start.6
  27.3 0.0 collective-permute-done.7.query_ref
  27.3 4.3 %collective-permute-start.9 = (bf16[5,96,128]{2,1,0:T(8,128)(2,1)S(1)}, bf16[5,96,128]{2,1,0:T(8,128)(2,1)S(1)}, u32[]{:S(2)}, u32[]{:S(2)}) collective-permute-start(bf16[5,96,128]{2,1,0:T(8,128)(2,1)S(1)} %get-tuple-element.19), channel_id=1, source_target_pairs={{0,16},{4,20},{8,24},{12,28},{16,0},{20,4},{24,8},{28,12},{1,17},{... | collective-permute-start | bytes 368648 | tf_op jit(solution)/shard_map/ppermute | solution.py:186
  31.6 0.0 collective-permute-done.3.refs_4_
  31.6 3.4 %collective-permute-start.11 = (bf16[5,96,128]{2,1,0:T(8,128)(2,1)S(1)}, bf16[5,96,128]{2,1,0:T(8,128)(2,1)S(1)}, u32[]{:S(2)}, u32[]{:S(2)}) collective-permute-start(bf16[5,96,128]{2,1,0:T(8,128)(2,1)S(1)} %get-tuple-element.20), channel_id=1, source_target_pairs={{0,24},{4,28},{8,0},{12,4},{16,8},{20,12},{24,16},{28,20},{1,25},{... | collective-permute-start | bytes 368648 | tf_op jit(solution)/shard_map/ppermute | solution.py:186
  35.0 0.1 reshape.60.tile_ref
  35.1 0.0 collective-permute-done.4.refs_5_
  35.1 2.4 %attend.5 = bf16[5,96,128]{2,1,0:T(8,128)(2,1)S(1)} custom-call(s32[1,96]{1,0:T(1,128)S(1)} %get-tuple-element.23.place_ref, s32[1,768]{1,0:T(1,128)S(1)} %reshape.60.tile_ref, bf16[5,96,128]{2,1,0:T(8,128)(2,1)S(1)} %collective-permute-done.7.query_ref, bf16[968,128]{1,0:T(8,128)(2,1)S(1)} %get-tuple-element.14.refs_0_, ...), custom_call_target="tpu_custom_call" | custom-call | flops 188743680 | bytes 2211840 | tf_op jit(solution)/shard_map/attend/pallas_call | solution.py:238
  37.5 0.4 collective-permute-start.8
  37.9 2.4 %attend.6 = bf16[5,96,128]{2,1,0:T(8,128)(2,1)S(1)} custom-call(s32[1,96]{1,0:T(1,128)S(1)} %get-tuple-element.22.place_ref, s32[1,768]{1,0:T(1,128)S(1)} %reshape.60.tile_ref, bf16[5,96,128]{2,1,0:T(8,128)(2,1)S(1)} %collective-permute-done.9.query_ref, bf16[968,128]{1,0:T(8,128)(2,1)S(1)} %get-tuple-element.14.refs_0_, ...), custom_call_target="tpu_custom_call" | custom-call | flops 188743680 | bytes 2211840 | tf_op jit(solution)/shard_map/attend/pallas_call | solution.py:238
  40.3 1.0 %collective-permute-start.10 = (bf16[5,96,128]{2,1,0:T(8,128)(2,1)S(1)}, bf16[5,96,128]{2,1,0:T(8,128)(2,1)S(1)}, u32[]{:S(2)}, u32[]{:S(2)}) collective-permute-start(bf16[5,96,128]{2,1,0:T(8,128)(2,1)S(1)} %attend.6), channel_id=1, source_target_pairs={{0,16},{4,20},{8,24},{12,28},{16,0},{20,4},{24,8},{28,12},{1,17},{... | collective-permute-start | bytes 368648 | tf_op jit(solution)/shard_map/ppermute | solution.py:186
  41.3 2.4 %attend.7 = bf16[5,96,128]{2,1,0:T(8,128)(2,1)S(1)} custom-call(s32[1,96]{1,0:T(1,128)S(1)} %get-tuple-element.21.place_ref, s32[1,768]{1,0:T(1,128)S(1)} %reshape.60.tile_ref, bf16[5,96,128]{2,1,0:T(8,128)(2,1)S(1)} %collective-permute-done.11.query_ref, bf16[968,128]{1,0:T(8,128)(2,1)S(1)} %get-tuple-element.14.refs_0_, ...), custom_call_target="tpu_custom_call" | custom-call | flops 188743680 | bytes 2211840 | tf_op jit(solution)/shard_map/attend/pallas_call | solution.py:238
  43.7 11.4 %collective-permute-start.12 = (bf16[5,96,128]{2,1,0:T(8,128)(2,1)S(1)}, bf16[5,96,128]{2,1,0:T(8,128)(2,1)S(1)}, u32[]{:S(2)}, u32[]{:S(2)}) collective-permute-start(bf16[5,96,128]{2,1,0:T(8,128)(2,1)S(1)} %attend.7), channel_id=1, source_target_pairs={{0,8},{4,12},{8,16},{12,20},{16,24},{20,28},{24,0},{28,4},{1,9},{5... | collective-permute-start | bytes 368648 | tf_op jit(solution)/shard_map/ppermute | solution.py:186
  55.1 2.4 %attend.4.refs_0_ = bf16[5,96,128]{2,1,0:T(8,128)(2,1)S(1)} custom-call(s32[1,96]{1,0:T(1,128)S(1)} %get-tuple-element.24.place_ref, s32[1,768]{1,0:T(1,128)S(1)} %reshape.60.tile_ref, bf16[5,96,128]{2,1,0:T(8,128)(2,1)S(1)} %get-tuple-element.13.query_ref, bf16[968,128]{1,0:T(8,128)(2,1)S(1)} %get-tuple-element.14.refs_0_, ...), custom_call_target="tpu_custom_call" | custom-call | flops 188743680 | bytes 2211840 | tf_op jit(solution)/shard_map/attend/pallas_call | solution.py:238
  57.5 0.7 %collective-permute-done.12.refs_3_ = bf16[5,96,128]{2,1,0:T(8,128)(2,1)S(1)} collective-permute-done((bf16[5,96,128]{2,1,0:T(8,128)(2,1)S(1)}, bf16[5,96,128]{2,1,0:T(8,128)(2,1)S(1)}, u32[]{:S(2)}, u32[]{:S(2)}) %collective-permute-start.12) | collective-permute-done | bytes 122912 | tf_op jit(solution)/shard_map/ppermute | solution.py:186
  58.3 1.4 %unpack.1 = bf16[96,2560]{1,0:T(8,128)(2,1)} custom-call(s32[4]{0:T(128)S(1)} %pad_add_fusion.offs, bf16[5,96,128]{2,1,0:T(8,128)(2,1)S(1)} %attend.4.refs_0_, bf16[5,96,128]{2,1,0:T(8,128)(2,1)S(1)} %collective-permute-done.8.refs_1_, bf16[5,96,128]{2,1,0:T(8,128)(2,1)S(1)} %collective-permute-done.10.refs_2_, ...), custom_call_target="tpu_custom_call" | custom-call | tf_op jit(solution)/shard_map/unpack/pallas_call | solution.py:240
  (23 shorter events, 0.1 us)
Async XLA Ops:
  0.1 1.0 %copy-start = (bf16[96,2560]{1,0:T(8,128)(2,1)S(1)}, bf16[96,2560]{1,0:T(8,128)(2,1)}, u32[]{:S(2)}) copy-start(bf16[96,2560]{1,0:T(8,128)(2,1)} %query_ref.1) | copy-start | bytes 1474564
  1.1 3.8 %copy-start.1 = (bf16[96,2560]{1,0:T(8,128)(2,1)S(1)}, bf16[96,2560]{1,0:T(8,128)(2,1)}, u32[]{:S(2)}) copy-start(bf16[96,2560]{1,0:T(8,128)(2,1)} %key_ref.1) | copy-start | bytes 1474564
  1.8 3.1 %copy-start.3 = (s32[2,4]{1,0:T(2,128)S(1)}, s32[2,4]{1,0:T(2,128)}, u32[]{:S(2)}) copy-start(s32[2,4]{1,0:T(2,128)} %tiles.1) | copy-start | bytes 100
  1.8 3.1 %copy-start.4 = (s32[2]{0:T(128)S(1)}, s32[2]{0:T(128)}, u32[]{:S(2)}) copy-start(s32[2]{0:T(128)} %count.1) | copy-start | bytes 28
  1.8 25.5 %collective-permute-start.7 = (bf16[5,96,128]{2,1,0:T(8,128)(2,1)S(1)}, bf16[5,96,128]{2,1,0:T(8,128)(2,1)S(1)}, u32[]{:S(2)}, u32[]{:S(2)}) collective-permute-start(bf16[5,96,128]{2,1,0:T(8,128)(2,1)S(1)} %get-tuple-element.18), channel_id=1, source_target_pairs={{0,8},{4,12},{8,16},{12,20},{16,24},{20,28},{24,0},{28,4},{1,9},{5... | collective-permute-start | bytes 368648 | tf_op jit(solution)/shard_map/ppermute | solution.py:186
  4.9 1.0 %copy-start.2 = (bf16[96,2560]{1,0:T(8,128)(2,1)S(1)}, bf16[96,2560]{1,0:T(8,128)(2,1)}, u32[]{:S(2)}) copy-start(bf16[96,2560]{1,0:T(8,128)(2,1)} %value_ref.1) | copy-start | bytes 1474564
  6.7 10.9 %collective-permute-start = (bf16[968,128]{1,0:T(8,128)(2,1)S(1)}, bf16[968,128]{1,0:T(8,128)(2,1)S(1)}, u32[]{:S(2)}, u32[]{:S(2)}) collective-permute-start(bf16[968,128]{1,0:T(8,128)(2,1)S(1)} %get-tuple-element.15), channel_id=1, source_target_pairs={{0,8},{4,12},{8,16},{12,20},{16,24},{20,28},{24,0},{28,4},{1,9},{5... | collective-permute-start | bytes 743432 | tf_op jit(solution)/shard_map/ppermute | solution.py:186
  8.3 18.4 %collective-permute-start.1 = (bf16[968,128]{1,0:T(8,128)(2,1)S(1)}, bf16[968,128]{1,0:T(8,128)(2,1)S(1)}, u32[]{:S(2)}, u32[]{:S(2)}) collective-permute-start(bf16[968,128]{1,0:T(8,128)(2,1)S(1)} %get-tuple-element.16), channel_id=1, source_target_pairs={{0,16},{4,20},{8,24},{12,28},{16,0},{20,4},{24,8},{28,12},{1,17},{... | collective-permute-start | bytes 743432 | tf_op jit(solution)/shard_map/ppermute | solution.py:186
  10.0 2.3 %copy-start.5 = (s32[768]{0:T(1024)S(1)}, s32[768]{0:T(1024)}, u32[]{:S(2)}) copy-start(s32[768]{0:T(1024)} %param.9) | copy-start | bytes 9220
  10.0 16.8 %collective-permute-start.2 = (bf16[968,128]{1,0:T(8,128)(2,1)S(1)}, bf16[968,128]{1,0:T(8,128)(2,1)S(1)}, u32[]{:S(2)}, u32[]{:S(2)}) collective-permute-start(bf16[968,128]{1,0:T(8,128)(2,1)S(1)} %get-tuple-element.17), channel_id=1, source_target_pairs={{0,24},{4,28},{8,0},{12,4},{16,8},{20,12},{24,16},{28,20},{1,25},{... | collective-permute-start | bytes 743432 | tf_op jit(solution)/shard_map/ppermute | solution.py:186
  12.3 19.4 %collective-permute-start.3 = (bf16[968,128]{1,0:T(8,128)(2,1)S(1)}, bf16[968,128]{1,0:T(8,128)(2,1)S(1)}, u32[]{:S(2)}, u32[]{:S(2)}) collective-permute-start(bf16[968,128]{1,0:T(8,128)(2,1)S(1)} %get-tuple-element.14.refs_0_), channel_id=1, source_target_pairs={{0,4},{4,0},{8,12},{12,8},{16,20},{20,16},{24,28},{28,24},{1,5},{5... | collective-permute-start | bytes 743432 | tf_op jit(solution)/shard_map/ppermute | solution.py:189
  17.6 17.6 %collective-permute-start.4 = (bf16[968,128]{1,0:T(8,128)(2,1)S(1)}, bf16[968,128]{1,0:T(8,128)(2,1)S(1)}, u32[]{:S(2)}, u32[]{:S(2)}) collective-permute-start(bf16[968,128]{1,0:T(8,128)(2,1)S(1)} %collective-permute-done.refs_1_), channel_id=1, source_target_pairs={{0,4},{4,0},{8,12},{12,8},{16,20},{20,16},{24,28},{28,24},{1,5},{5... | collective-permute-start | bytes 743432 | tf_op jit(solution)/shard_map/ppermute | solution.py:189
  26.8 8.4 %collective-permute-start.5 = (bf16[968,128]{1,0:T(8,128)(2,1)S(1)}, bf16[968,128]{1,0:T(8,128)(2,1)S(1)}, u32[]{:S(2)}, u32[]{:S(2)}) collective-permute-start(bf16[968,128]{1,0:T(8,128)(2,1)S(1)} %collective-permute-done.1.refs_2_), channel_id=1, source_target_pairs={{0,4},{4,0},{8,12},{12,8},{16,20},{20,16},{24,28},{28,24},{1,5},{5... | collective-permute-start | bytes 743432 | tf_op jit(solution)/shard_map/ppermute | solution.py:189
  26.8 8.4 %collective-permute-start.6 = (bf16[968,128]{1,0:T(8,128)(2,1)S(1)}, bf16[968,128]{1,0:T(8,128)(2,1)S(1)}, u32[]{:S(2)}, u32[]{:S(2)}) collective-permute-start(bf16[968,128]{1,0:T(8,128)(2,1)S(1)} %collective-permute-done.2.refs_3_), channel_id=1, source_target_pairs={{0,4},{4,0},{8,12},{12,8},{16,20},{20,16},{24,28},{28,24},{1,5},{5... | collective-permute-start | bytes 743432 | tf_op jit(solution)/shard_map/ppermute | solution.py:189
  27.3 10.6 %collective-permute-start.9 = (bf16[5,96,128]{2,1,0:T(8,128)(2,1)S(1)}, bf16[5,96,128]{2,1,0:T(8,128)(2,1)S(1)}, u32[]{:S(2)}, u32[]{:S(2)}) collective-permute-start(bf16[5,96,128]{2,1,0:T(8,128)(2,1)S(1)} %get-tuple-element.19), channel_id=1, source_target_pairs={{0,16},{4,20},{8,24},{12,28},{16,0},{20,4},{24,8},{28,12},{1,17},{... | collective-permute-start | bytes 368648 | tf_op jit(solution)/shard_map/ppermute | solution.py:186
  31.6 9.7 %collective-permute-start.11 = (bf16[5,96,128]{2,1,0:T(8,128)(2,1)S(1)}, bf16[5,96,128]{2,1,0:T(8,128)(2,1)S(1)}, u32[]{:S(2)}, u32[]{:S(2)}) collective-permute-start(bf16[5,96,128]{2,1,0:T(8,128)(2,1)S(1)} %get-tuple-element.20), channel_id=1, source_target_pairs={{0,24},{4,28},{8,0},{12,4},{16,8},{20,12},{24,16},{28,20},{1,25},{... | collective-permute-start | bytes 368648 | tf_op jit(solution)/shard_map/ppermute | solution.py:186
  37.5 20.0 %collective-permute-start.8 = (bf16[5,96,128]{2,1,0:T(8,128)(2,1)S(1)}, bf16[5,96,128]{2,1,0:T(8,128)(2,1)S(1)}, u32[]{:S(2)}, u32[]{:S(2)}) collective-permute-start(bf16[5,96,128]{2,1,0:T(8,128)(2,1)S(1)} %attend.5), channel_id=1, source_target_pairs={{0,24},{4,28},{8,0},{12,4},{16,8},{20,12},{24,16},{28,20},{1,25},{... | collective-permute-start | bytes 368648 | tf_op jit(solution)/shard_map/ppermute | solution.py:186
  40.3 17.2 %collective-permute-start.10 = (bf16[5,96,128]{2,1,0:T(8,128)(2,1)S(1)}, bf16[5,96,128]{2,1,0:T(8,128)(2,1)S(1)}, u32[]{:S(2)}, u32[]{:S(2)}) collective-permute-start(bf16[5,96,128]{2,1,0:T(8,128)(2,1)S(1)} %attend.6), channel_id=1, source_target_pairs={{0,16},{4,20},{8,24},{12,28},{16,0},{20,4},{24,8},{28,12},{1,17},{... | collective-permute-start | bytes 368648 | tf_op jit(solution)/shard_map/ppermute | solution.py:186
  43.7 14.6 %collective-permute-start.12 = (bf16[5,96,128]{2,1,0:T(8,128)(2,1)S(1)}, bf16[5,96,128]{2,1,0:T(8,128)(2,1)S(1)}, u32[]{:S(2)}, u32[]{:S(2)}) collective-permute-start(bf16[5,96,128]{2,1,0:T(8,128)(2,1)S(1)} %attend.7), channel_id=1, source_target_pairs={{0,8},{4,12},{8,16},{12,20},{16,24},{20,28},{24,0},{28,4},{1,9},{5... | collective-permute-start | bytes 368648 | tf_op jit(solution)/shard_map/ppermute | solution.py:186

commit v2 on v0

--- a/solution.py
+++ b/solution.py
@@ -1,6 +1,10 @@
+import functools
+
 import jax
 import jax.numpy as jnp
 from jax import lax
+from jax.experimental import pallas as pl
+from jax.experimental.pallas import tpu as pltpu
 from jax.sharding import PartitionSpec as P
 
 HD = 128
@@ -89,9 +93,270 @@
     return arrived_back.reshape(rows_dev, feat_width)[jnp.argsort(send_order)]
 
 
+LATE = 2
+META = 8
+MASKED = -1e30
+LOG2E = 1.4426950408889634
+VMEM = pltpu.VMEM
+SMEM = pltpu.SMEM
+
+
+def whole(space=VMEM):
+    return pl.BlockSpec(memory_space=space)
+
+
+def params():
+    return pltpu.CompilerParams(vmem_limit_bytes=16 << 20)
+
+
+@functools.cache
+def rounds_of(chips):
+    steps = range(1, chips)
+    if chips & (chips - 1) == 0:
+        rounds = [tuple(c ^ by for c in range(chips)) for by in steps]
+    else:
+        rounds = [tuple((c + by) % chips for c in range(chips)) for by in steps]
+
+    return tuple(rounds[::-1])
+
+
+def inverse_of(perm):
+    return tuple(perm.index(c) for c in range(len(perm)))
+
+
+def by_chip(table, chip):
+    value = jnp.int32(table[0])
+    for c, entry in enumerate(table[1:], 1):
+        value = jnp.where(chip == c, entry, value)
+    return value
+
+
+def pack_kernel(dest, heads, parts, tiles_hbm, count_hbm, query_ref, key_ref, value_ref, *refs):
+    outs, (tiles, count, sem, small_sem) = refs[:-4], refs[-4:]
+    rows = query_ref.shape[0]
+    chip = lax.axis_index("seq") // 2
+    lists = [
+        pltpu.make_async_copy(tiles_hbm, tiles, small_sem),
+        pltpu.make_async_copy(count_hbm, count, small_sem),
+    ]
+    for item in lists:
+        item.start()
+    copies = []
+    for (r, chosen), out in zip(parts, outs):
+        base = by_chip(dest[r], chip) * (heads * HD)
+        for i, h in enumerate(chosen):
+            cols = pl.ds(pl.multiple_of(base + h * HD, HD), HD)
+            for j, ref in enumerate((query_ref, key_ref, value_ref)):
+                target = out.at[pl.ds((3 * i + j) * rows, rows), :]
+                copies.append(pltpu.make_async_copy(ref.at[:, cols], target, sem))
+                copies[-1].start()
+    for item in lists:
+        item.wait()
+    row = lax.broadcasted_iota(jnp.int32, (META, HD), 0)
+    lane = lax.broadcasted_iota(jnp.int32, (META, HD), 1)
+    listed = jnp.zeros((META, HD), jnp.bool_)
+    for t in range(tiles.shape[0]):
+        for m in range(tiles.shape[1]):
+            entry = jnp.where(m < count[t], tiles[t, m], -1)
+            listed = listed | ((row == t) & (lane == entry))
+    meta = jnp.where(listed, 1.0, 0.0).astype(jnp.bfloat16)
+    for (r, chosen), out in zip(parts, outs):
+        if 0 in chosen:
+            out[pl.ds(3 * len(chosen) * rows, META), :] = meta
+    for item in copies:
+        item.wait()
+
+
+def mask_kernel(blocks, heads, place_ref, tile_ref, *refs):
+    got, deny_ref, owner_ref = refs[:blocks], refs[blocks], refs[blocks + 1]
+    rows = place_ref.shape[1]
+    lists = jnp.concatenate([r[pl.ds(3 * heads * rows, META), :] for r in got], axis=0)
+    row = lax.broadcasted_iota(jnp.int32, (blocks * META, rows), 0)
+    first = (((0,), (0,)), ((), ()))
+    for r in range(place_ref.shape[0]):
+        place = jnp.where(row == place_ref[pl.ds(r, 1), :], 1.0, 0.0).astype(jnp.bfloat16)
+        mine = lax.dot_general(place, lists, first, preferred_element_type=jnp.float32)
+        deny_ref[r] = jnp.where(mine > 0.5, 0.0, MASKED).astype(jnp.bfloat16)
+    tile = lax.broadcasted_iota(jnp.int32, (HD, tile_ref.shape[1]), 0) == tile_ref[...]
+    same = lax.broadcasted_iota(jnp.int32, (HD, HD), 0) == lax.broadcasted_iota(jnp.int32, (HD, HD), 1)
+    owner_ref[...] = lax.dot_general(
+        jnp.where(tile, 1.0, 0.0).astype(jnp.bfloat16),
+        jnp.where(same, 1.0, 0.0).astype(jnp.bfloat16),
+        first, preferred_element_type=jnp.float32,
+    ).astype(jnp.bfloat16)
+
+
+def attend_kernel(blocks, index, deny_ref, owner_ref, *refs):
+    got, (out_ref, scores_ref, weights_ref) = refs[:blocks], refs[blocks:]
+    heads, rows = out_ref.shape[:2]
+    deny, owner = deny_ref[index], owner_ref[...]
+    ones = jnp.ones((blocks * rows, HD), jnp.bfloat16)
+
+    def joined(part, h, other):
+        at = pl.ds((3 * h + part) * rows, rows)
+        return jnp.concatenate([jnp.concatenate([r[at, :] for r in got], axis=0), other], axis=1)
+
+    for h in range(heads):
+        query = jnp.concatenate([got[index][pl.ds(3 * h * rows, rows), :], deny], axis=1)
+        scores_ref[h] = lax.dot_general(
+            query, joined(1, h, owner), (((1,), (1,)), ((), ())), preferred_element_type=jnp.float32
+        )
+    for h in range(heads):
+        scores = scores_ref[h]
+        peak = jnp.max(scores, axis=-1, keepdims=True)
+        weights_ref[h] = jnp.exp2((scores - peak) * (HD ** (-0.5) * LOG2E)).astype(jnp.bfloat16)
+    for h in range(heads):
+        mixed = jnp.dot(weights_ref[h], joined(2, h, ones), preferred_element_type=jnp.float32)
+        out_ref[h] = (mixed[:, :HD] / mixed[:, HD:]).astype(jnp.bfloat16)
+
+
+def unpack_kernel(dest, heads, chosen, aliased, *refs):
+    parts, out_ref, sem = refs[aliased : aliased + len(dest)], refs[-2], refs[-1]
+    chip = lax.axis_index("seq") // 2
+    copies = []
+    for r, part in enumerate(parts):
+        base = by_chip(dest[r], chip) * (heads * HD)
+        for i, h in enumerate(chosen):
+            cols = pl.ds(pl.multiple_of(base + h * HD, HD), HD)
+            copies.append(pltpu.make_async_copy(part.at[i], out_ref.at[:, cols], sem))
+            copies[-1].start()
+    for item in copies:
+        item.wait()
+
+
+def by_heads(query_proj, key_proj, value_proj, token_rows, key_tiles, key_count):
+    members = lax.axis_size("seq")
+    chips = members // 2
+    myself = lax.axis_index("seq")
+    chip, core = myself >> 1, myself & 1
+    rows, feat = query_proj.shape
+    heads = feat // HD // chips
+    tiles_dev = key_tiles.shape[0]
+    tile_rows = rows // tiles_dev
+    bf16 = jnp.bfloat16
+    dest = (tuple(range(chips)),) + rounds_of(chips)
+    came = tuple(inverse_of(perm) for perm in dest)
+    steps = range(chips)
+    late = max(0, min(LATE, heads - 1))
+    groups = [tuple(range(heads - late))] + ([tuple(range(heads - late, heads))] if late else [])
+
+    def sent(value, perm):
+        pairs = [(2 * a + k, 2 * b + k) for a, b in enumerate(perm) for k in range(2)]
+        return lax.ppermute(value, "seq", pairs)
+
+    def crossed(value):
+        return lax.ppermute(value, "seq", [(i, i ^ 1) for i in range(members)])
+
+    operands = [
+        pltpu.with_memory_space_constraint(x, pltpu.HBM)
+        for x in (key_tiles, key_count, query_proj, key_proj, value_proj)
+    ]
+
+    def pack(parts):
+        return pl.pallas_call(
+            functools.partial(pack_kernel, dest, heads, parts),
+            out_shape=[
+                jax.ShapeDtypeStruct((3 * len(chosen) * rows + META * (0 in chosen), HD), bf16)
+                for r, chosen in parts
+            ],
+            in_specs=[whole(pltpu.HBM)] * 5,
+            out_specs=[whole()] * len(parts),
+            scratch_shapes=[
+                SMEM(key_tiles.shape, jnp.int32),
+                SMEM(key_count.shape, jnp.int32),
+                pltpu.SemaphoreType.DMA,
+                pltpu.SemaphoreType.DMA,
+            ],
+            compiler_params=params(),
+        )(*operands)
+
+    parts = [(r, chosen) for chosen in groups for r in (*steps[1:], 0)]
+    packed = dict(zip(parts[:1], pack(parts[:1])))
+    packed.update(zip(parts[1:], pack(parts[1:])))
+    got = []
+    for g, chosen in enumerate(groups):
+        here = [packed[0, chosen]] + [sent(packed[r, chosen], dest[r]) for r in steps[1:]]
+        got.append(here + [crossed(value) for value in here])
+
+    slab_tiles = (token_rows // tile_rows).reshape(members, rows)
+    source_chip = jnp.stack([by_chip(table, chip) for table in came])
+    source = jnp.concatenate([source_chip * 2 + core, source_chip * 2 + 1 - core])
+    block_tiles = slab_tiles[source]
+    key_tile = block_tiles.reshape(1, members * rows)
+    owner = block_tiles[:chips] // tiles_dev
+    arrived = jnp.sum(
+        jnp.where(source_chip == (owner >> 1)[..., None], jnp.arange(chips), 0), axis=-1
+    )
+    place = (arrived + jnp.where((owner & 1) == core, 0, chips)) * META
+    place = place + block_tiles[:chips] % tiles_dev
+    deny, owned = pl.pallas_call(
+        functools.partial(mask_kernel, members, len(groups[0])),
+        out_shape=[
+            jax.ShapeDtypeStruct((chips, rows, HD), bf16),
+            jax.ShapeDtypeStruct((members * rows, HD), bf16),
+        ],
+        in_specs=[whole()] * (2 + members),
+        out_specs=[whole()] * 2,
+        compiler_params=params(),
+        name="mask",
+    )(place, key_tile, *got[0])
+
+    result = None
+    for g, chosen in enumerate(groups):
+        count = len(chosen)
+
+        def attend(r):
+            return pl.pallas_call(
+                functools.partial(attend_kernel, members, r),
+                out_shape=jax.ShapeDtypeStruct((count, rows, HD), bf16),
+                in_specs=[whole()] * (2 + members),
+                out_specs=whole(),
+                scratch_shapes=[
+                    VMEM((count, rows, members * rows), jnp.float32),
+                    VMEM((count, rows, members * rows), bf16),
+                ],
+                compiler_params=params(),
+                cost_estimate=pl.CostEstimate(
+                    flops=4 * count * rows * rows * members * HD,
+                    bytes_accessed=6 * count * rows * HD * members,
+                    transcendentals=count * rows * rows * members,
+                ),
+            )(deny, owned, *got[g])
+
+        outs = [attend(r) for r in steps]
+        back = [outs[0]] + [sent(outs[r], came[r]) for r in steps[1:]]
+        carried = [] if result is None else [result]
+        result = pl.pallas_call(
+            functools.partial(unpack_kernel, dest, heads, chosen, len(carried)),
+            out_shape=jax.ShapeDtypeStruct((rows, feat), bf16),
+            in_specs=[whole(pltpu.HBM)] * len(carried) + [whole()] * chips,
+            out_specs=whole(pltpu.HBM),
+            scratch_shapes=[pltpu.SemaphoreType.DMA],
+            input_output_aliases={0: 0} if carried else {},
+            compiler_params=params(),
+        )(*carried, *back)
+    return result
+
+
+def shards_of(*args):
+    members = lax.axis_size("seq")
+    rows, feat = args[0].shape
+    chips = members // 2
+    tiles = args[4].shape[0]
+    if (
+        members % 2 == 0
+        and feat // HD % chips == 0
+        and rows % 16 == 0
+        and tiles <= META
+        and tiles * members <= HD
+    ):
+        return by_heads(*args)
+    return shards(*args)
+
+
 def solution(mesh):
     return jax.shard_map(
-        shards,
+        shards_of,
         mesh=mesh,
         in_specs=(
             P(("dp", "seq"), None),

time: 229 us -> 63 us (0.28)
  matrix products: 47.2 us -> 0 us
  local copies, waits for them, and re-layouts: 38.8 us -> 1.39 us
  waiting for transfers between devices: 65 us -> 30.6 us
  starting transfers between devices: 41.8 us -> 20.3 us
  other arithmetic: 19.6 us -> 0.3 us
  loops' own time: 14 us -> 0 us
  Pallas kernels: 0 us -> 9.97 us
    dot_general x40 -> x0, matrix products: 47.2 us -> none  [the longest x20 24.2 us: one_head(): jnp.einsum('...qd,...kd->...qk', query_head, key_head, preferred_element_...]
    all_to_all x4 -> x0, waiting for transfers between devices: 46.1 us -> none  [the longest x1 16.3 us: shards(): lax.all_to_all(sorted_values, 'seq', split_axis=0, concat_axis=0, tiled=T...]
    all_to_all x4 -> x0, starting transfers between devices: 22.2 us -> none  [the longest x1 8.77 us: shards(): lax.all_to_all(back_send, 'seq', split_axis=0, concat_axis=0, tiled=True)]
    sort x5 -> x0, other arithmetic: 15.3 us -> none  [the longest x1 5.11 us: shards(): inverse = jnp.argsort(token_rows)]
    another operation x1 -> x0, loops' own time: 14 us -> none  [attend_heads(): return lax.map(one_head, jnp.arange(head_count))]
    dynamic_slice x21 -> x0, local copies, waits for them, and re-layouts: 12.5 us -> none  [the longest x20 11.7 us: attend_heads(): return lax.map(one_head, jnp.arange(head_count))]
    ppermute x8 -> x20, waiting for transfers between devices: 18.9 us -> 30.6 us  [the longest x12 29.3 us: sent(): return lax.ppermute(value, 'seq', pairs)]
    pallas_call x0 -> x13, Pallas kernels: none -> 9.97 us  [the longest x8 6.09 us: attend(): pl.pallas_call(functools.partial(attend_kernel, members, r), out_shape=ja...]
  transfers between devices with their start and end apart: 12 -> 20, of which waited for: 7 -> 6; matrix products, arithmetic and copies ran while one was open for 10% -> 2% of each run, Pallas kernels for 0% -> 13%
where the time goes in v2:
time: 63 us; the launch traced here: 62.7 us
  waiting for transfers between devices  30.6 us (49%)
  starting transfers between devices  20.3 us (32%)
  Pallas kernels  9.97 us (16%)
  local copies, waits for them, and re-layouts  1.39 us (2%)
    ppermute x12, waiting for transfers between devices, sent(): return lax.ppermute(value, 'seq', pairs)  29.3 us
    ppermute x12, starting transfers between devices, sent(): return lax.ppermute(value, 'seq', pairs)  18.7 us
    pallas_call x8, Pallas kernels, attend(): pl.pallas_call(functools.partial(attend_kernel, members, r), out_shape=ja...  6.09 us
    pallas_call x2, Pallas kernels, pack(): pl.pallas_call(functools.partial(pack_kernel, dest, heads, parts), out_sh...  2.21 us
    ppermute x8, starting transfers between devices, crossed(): return lax.ppermute(value, 'seq', [(i, i ^ 1) for i in range(members)])  1.59 us
    pallas_call x2, Pallas kernels, by_heads(): pl.pallas_call(functools.partial(unpack_kernel, dest, heads, chosen, len(...  1.4 us
    ppermute x8, waiting for transfers between devices, crossed(): return lax.ppermute(value, 'seq', [(i, i ^ 1) for i in range(members)])  1.33 us
  transfers between devices with their start and end apart: 20, of which 6 were waited for; matrix products, arithmetic and copies ran while one was open for 2% of the time, Pallas kernels for 13%

profile of v2, /device:TPU:0, one launch (start us, length us, event | category | flops | bytes accessed | tf_op | source)
XLA Modules:
  0.0 62.7 jit_solution(15617019602391406593)
XLA Ops:
  0.0 0.9 %shard_map.65 = bf16[872,128]{1,0:T(8,128)(2,1)S(1)} custom-call(s32[2,4]{1,0:T(2,128)} %tiles_hbm.3, s32[2]{0:T(128)} %count_hbm.3, bf16[96,2560]{1,0:T(8,128)(2,1)} %query_ref.3, bf16[96,2560]{1,0:T(8,128)(2,1)} %key_ref.3, bf16[96,2560]{1,0:T(8,128)(2,1)} %value_ref.3), custom_call_target="tpu_custom_call" | custom-call | tf_op jit(solution)/shard_map/pallas_call | solution.py:256
  0.9 5.1 %collective-permute-start = (bf16[872,128]{1,0:T(8,128)(2,1)S(1)}, bf16[872,128]{1,0:T(8,128)(2,1)S(1)}, u32[]{:S(2)}, u32[]{:S(2)}) collective-permute-start(bf16[872,128]{1,0:T(8,128)(2,1)S(1)} %shard_map.65), channel_id=1, source_target_pairs={{0,24},{4,28},{8,16},{12,20},{16,8},{20,12},{24,0},{28,4},{1,25},{... | collective-permute-start | bytes 669704 | tf_op jit(solution)/shard_map/ppermute | solution.py:245
  6.0 1.3 %shard_map.64 = (bf16[872,128]{1,0:T(8,128)(2,1)S(1)}, bf16[872,128]{1,0:T(8,128)(2,1)S(1)}, bf16[872,128]{1,0:T(8,128)(2,1)S(1)}, bf16[576,128]{1,0:T(8,128)(2,...) custom-call(s32[2,4]{1,0:T(2,128)} %tiles_hbm.3, s32[2]{0:T(128)} %count_hbm.3, ...), custom_call_target="tpu_custom_call" | custom-call | tf_op jit(solution)/shard_map/pallas_call | solution.py:256
  7.4 0.6 collective-permute-start.2
  8.0 3.8 %collective-permute-start.10 = (bf16[576,128]{1,0:T(8,128)(2,1)S(1)}, bf16[576,128]{1,0:T(8,128)(2,1)S(1)}, u32[]{:S(2)}, u32[]{:S(2)}) collective-permute-start(bf16[576,128]{1,0:T(8,128)(2,1)S(1)} %get-tuple-element.20), channel_id=1, source_target_pairs={{0,24},{4,28},{8,16},{12,20},{16,8},{20,12},{24,0},{28,4},{1,25},{... | collective-permute-start | bytes 442376 | tf_op jit(solution)/shard_map/ppermute | solution.py:245
  11.8 0.7 %copy-done = s32[768]{0:T(1024)S(1)} copy-done((s32[768]{0:T(1024)S(1)}, s32[768]{0:T(1024)}, u32[]{:S(2)}) %copy-start) | copy-done | bytes 3096
  12.8 0.6 gather_fusion
  13.4 11.9 %collective-permute-done.10.refs_1_ = bf16[576,128]{1,0:T(8,128)(2,1)S(1)} collective-permute-done((bf16[576,128]{1,0:T(8,128)(2,1)S(1)}, bf16[576,128]{1,0:T(8,128)(2,1)S(1)}, u32[]{:S(2)}, u32[]{:S(2)}) %collective-permute-start.10) | collective-permute-done | bytes 147488 | tf_op jit(solution)/shard_map/ppermute | solution.py:245
  25.2 12.4 %collective-permute-done.11.refs_2_ = bf16[576,128]{1,0:T(8,128)(2,1)S(1)} collective-permute-done((bf16[576,128]{1,0:T(8,128)(2,1)S(1)}, bf16[576,128]{1,0:T(8,128)(2,1)S(1)}, u32[]{:S(2)}, u32[]{:S(2)}) %collective-permute-start.11) | collective-permute-done | bytes 147488 | tf_op jit(solution)/shard_map/ppermute | solution.py:245
  37.7 0.5 collective-permute-start.5
  38.2 0.1 select_reduce_fusion
  38.3 4.5 %collective-permute-done.12.refs_3_ = bf16[576,128]{1,0:T(8,128)(2,1)S(1)} collective-permute-done((bf16[576,128]{1,0:T(8,128)(2,1)S(1)}, bf16[576,128]{1,0:T(8,128)(2,1)S(1)}, u32[]{:S(2)}, u32[]{:S(2)}) %collective-permute-start.12) | collective-permute-done | bytes 147488 | tf_op jit(solution)/shard_map/ppermute | solution.py:245
  42.8 0.5 collective-permute-start.14
  43.4 0.4 collective-permute-start.16
  44.0 1.3 %collective-permute-done.6.refs_7_ = bf16[872,128]{1,0:T(8,128)(2,1)S(1)} collective-permute-done((bf16[872,128]{1,0:T(8,128)(2,1)S(1)}, bf16[872,128]{1,0:T(8,128)(2,1)S(1)}, u32[]{:S(2)}, u32[]{:S(2)}) %collective-permute-start.6) | collective-permute-done | bytes 223264 | tf_op jit(solution)/shard_map/ppermute | solution.py:248
  45.3 0.3 mask.1
  45.6 0.8 %shard_map.67 = bf16[3,96,128]{2,1,0:T(8,128)(2,1)S(1)} custom-call(bf16[4,96,128]{2,1,0:T(8,128)(2,1)S(1)} %get-tuple-element.17.deny_ref, bf16[768,128]{1,0:T(8,128)(2,1)S(1)} %get-tuple-element.18.owner_ref, bf16[872,128]{1,0:T(8,128)(2,1)S(1)} %get-tuple-element.14.refs_0_, bf16[872,128]{1,0:T(8,128)(2,1)S(1)} %collective-permute-done.refs_1_, ...), custom_call_target="tpu_custom_call" | custom-call | flops 113246208 | bytes 1769472 | tf_op jit(solution)/shard_map/pallas_call | solution.py:309
  46.4 2.5 %collective-permute-start.7 = (bf16[3,96,128]{2,1,0:T(8,128)(2,1)S(1)}, bf16[3,96,128]{2,1,0:T(8,128)(2,1)S(1)}, u32[]{:S(2)}, u32[]{:S(2)}) collective-permute-start(bf16[3,96,128]{2,1,0:T(8,128)(2,1)S(1)} %shard_map.67), channel_id=1, source_target_pairs={{0,24},{4,28},{8,16},{12,20},{16,8},{20,12},{24,0},{28,4},{1,25},{... | collective-permute-start | bytes 221192 | tf_op jit(solution)/shard_map/ppermute | solution.py:245
  49.0 0.8 %shard_map.68 = bf16[3,96,128]{2,1,0:T(8,128)(2,1)S(1)} custom-call(bf16[4,96,128]{2,1,0:T(8,128)(2,1)S(1)} %get-tuple-element.17.deny_ref, bf16[768,128]{1,0:T(8,128)(2,1)S(1)} %get-tuple-element.18.owner_ref, bf16[872,128]{1,0:T(8,128)(2,1)S(1)} %get-tuple-element.14.refs_0_, bf16[872,128]{1,0:T(8,128)(2,1)S(1)} %collective-permute-done.refs_1_, ...), custom_call_target="tpu_custom_call" | custom-call | flops 113246208 | bytes 1769472 | tf_op jit(solution)/shard_map/pallas_call | solution.py:309
  49.8 0.8 %shard_map.69 = bf16[3,96,128]{2,1,0:T(8,128)(2,1)S(1)} custom-call(bf16[4,96,128]{2,1,0:T(8,128)(2,1)S(1)} %get-tuple-element.17.deny_ref, bf16[768,128]{1,0:T(8,128)(2,1)S(1)} %get-tuple-element.18.owner_ref, bf16[872,128]{1,0:T(8,128)(2,1)S(1)} %get-tuple-element.14.refs_0_, bf16[872,128]{1,0:T(8,128)(2,1)S(1)} %collective-permute-done.refs_1_, ...), custom_call_target="tpu_custom_call" | custom-call | flops 113246208 | bytes 1769472 | tf_op jit(solution)/shard_map/pallas_call | solution.py:309
  50.7 1.9 %collective-permute-start.9 = (bf16[3,96,128]{2,1,0:T(8,128)(2,1)S(1)}, bf16[3,96,128]{2,1,0:T(8,128)(2,1)S(1)}, u32[]{:S(2)}, u32[]{:S(2)}) collective-permute-start(bf16[3,96,128]{2,1,0:T(8,128)(2,1)S(1)} %shard_map.69), channel_id=1, source_target_pairs={{0,8},{4,12},{8,0},{12,4},{16,24},{20,28},{24,16},{28,20},{1,9},{5... | collective-permute-start | bytes 221192 | tf_op jit(solution)/shard_map/ppermute | solution.py:245
  52.6 0.7 %shard_map.72 = bf16[2,96,128]{2,1,0:T(8,128)(2,1)S(1)} custom-call(bf16[4,96,128]{2,1,0:T(8,128)(2,1)S(1)} %get-tuple-element.17.deny_ref, bf16[768,128]{1,0:T(8,128)(2,1)S(1)} %get-tuple-element.18.owner_ref, bf16[576,128]{1,0:T(8,128)(2,1)S(1)} %get-tuple-element.19.refs_0_, bf16[576,128]{1,0:T(8,128)(2,1)S(1)} %collective-permute-done.10.refs_1_, ...), custom_call_target="tpu_custom_call" | custom-call | flops 75497472 | bytes 1179648 | tf_op jit(solution)/shard_map/pallas_call | solution.py:309
  53.3 2.5 %collective-permute-start.17 = (bf16[2,96,128]{2,1,0:T(8,128)(2,1)S(1)}, bf16[2,96,128]{2,1,0:T(8,128)(2,1)S(1)}, u32[]{:S(2)}, u32[]{:S(2)}) collective-permute-start(bf16[2,96,128]{2,1,0:T(8,128)(2,1)S(1)} %shard_map.72), channel_id=1, source_target_pairs={{0,24},{4,28},{8,16},{12,20},{16,8},{20,12},{24,0},{28,4},{1,25},{... | collective-permute-start | bytes 147464 | tf_op jit(solution)/shard_map/ppermute | solution.py:245
  55.9 0.7 %shard_map.73 = bf16[2,96,128]{2,1,0:T(8,128)(2,1)S(1)} custom-call(bf16[4,96,128]{2,1,0:T(8,128)(2,1)S(1)} %get-tuple-element.17.deny_ref, bf16[768,128]{1,0:T(8,128)(2,1)S(1)} %get-tuple-element.18.owner_ref, bf16[576,128]{1,0:T(8,128)(2,1)S(1)} %get-tuple-element.19.refs_0_, bf16[576,128]{1,0:T(8,128)(2,1)S(1)} %collective-permute-done.10.refs_1_, ...), custom_call_target="tpu_custom_call" | custom-call | flops 75497472 | bytes 1179648 | tf_op jit(solution)/shard_map/pallas_call | solution.py:309
  56.7 0.7 %shard_map.74 = bf16[2,96,128]{2,1,0:T(8,128)(2,1)S(1)} custom-call(bf16[4,96,128]{2,1,0:T(8,128)(2,1)S(1)} %get-tuple-element.17.deny_ref, bf16[768,128]{1,0:T(8,128)(2,1)S(1)} %get-tuple-element.18.owner_ref, bf16[576,128]{1,0:T(8,128)(2,1)S(1)} %get-tuple-element.19.refs_0_, bf16[576,128]{1,0:T(8,128)(2,1)S(1)} %collective-permute-done.10.refs_1_, ...), custom_call_target="tpu_custom_call" | custom-call | flops 75497472 | bytes 1179648 | tf_op jit(solution)/shard_map/pallas_call | solution.py:309
  57.4 2.0 %collective-permute-start.19 = (bf16[2,96,128]{2,1,0:T(8,128)(2,1)S(1)}, bf16[2,96,128]{2,1,0:T(8,128)(2,1)S(1)}, u32[]{:S(2)}, u32[]{:S(2)}) collective-permute-start(bf16[2,96,128]{2,1,0:T(8,128)(2,1)S(1)} %shard_map.74), channel_id=1, source_target_pairs={{0,8},{4,12},{8,0},{12,4},{16,24},{20,28},{24,16},{28,20},{1,9},{5... | collective-permute-start | bytes 147464 | tf_op jit(solution)/shard_map/ppermute | solution.py:245
  59.3 0.7 %shard_map.71.refs_1_ = bf16[2,96,128]{2,1,0:T(8,128)(2,1)S(1)} custom-call(bf16[4,96,128]{2,1,0:T(8,128)(2,1)S(1)} %get-tuple-element.17.deny_ref, bf16[768,128]{1,0:T(8,128)(2,1)S(1)} %get-tuple-element.18.owner_ref, bf16[576,128]{1,0:T(8,128)(2,1)S(1)} %get-tuple-element.19.refs_0_, bf16[576,128]{1,0:T(8,128)(2,1)S(1)} %collective-permute-done.10.refs_1_, ...), custom_call_target="tpu_custom_call" | custom-call | flops 75497472 | bytes 1179648 | tf_op jit(solution)/shard_map/pallas_call | solution.py:309
  60.0 0.8 %shard_map.66.refs_0_ = bf16[3,96,128]{2,1,0:T(8,128)(2,1)S(1)} custom-call(bf16[4,96,128]{2,1,0:T(8,128)(2,1)S(1)} %get-tuple-element.17.deny_ref, bf16[768,128]{1,0:T(8,128)(2,1)S(1)} %get-tuple-element.18.owner_ref, bf16[872,128]{1,0:T(8,128)(2,1)S(1)} %get-tuple-element.14.refs_0_, bf16[872,128]{1,0:T(8,128)(2,1)S(1)} %collective-permute-done.refs_1_, ...), custom_call_target="tpu_custom_call" | custom-call | flops 113246208 | bytes 1769472 | tf_op jit(solution)/shard_map/pallas_call | solution.py:309
  60.9 0.7 %shard_map.70.refs_0_ = bf16[96,2560]{1,0:T(8,128)(2,1)} custom-call(bf16[3,96,128]{2,1,0:T(8,128)(2,1)S(1)} %shard_map.66.refs_0_, bf16[3,96,128]{2,1,0:T(8,128)(2,1)S(1)} %collective-permute-done.7.refs_1_, bf16[3,96,128]{2,1,0:T(8,128)(2,1)S(1)} %collective-permute-done.8.refs_2_, bf16[3,96,128]{2,1,0:T(8,128)(2,1)S(1)} %collective-permute-done.9.refs_3_), custom_call_target="tpu_custom_call" | custom-call | tf_op jit(solution)/shard_map/pallas_call | solution.py:329
  61.6 0.1 collective-permute-done.18.refs_3_
  61.7 0.3 collective-permute-done.19.refs_4_
  62.1 0.7 %shard_map.75 = bf16[96,2560]{1,0:T(8,128)(2,1)} custom-call(bf16[96,2560]{1,0:T(8,128)(2,1)} %shard_map.70.refs_0_, bf16[2,96,128]{2,1,0:T(8,128)(2,1)S(1)} %shard_map.71.refs_1_, bf16[2,96,128]{2,1,0:T(8,128)(2,1)S(1)} %collective-permute-done.17.refs_2_, bf16[2,96,128]{2,1,0:T(8,128)(2,1)S(1)} %collective-permute-done.18.refs_3_, ...), custom_call_target="tpu_custom_call", output_to_operand_aliasing={{}: (0, {})} | custom-call | tf_op jit(solution)/shard_map/pallas_call | solution.py:329
  (34 shorter events, 0.8 us)
Async XLA Ops:
  0.9 36.8 %collective-permute-start = (bf16[872,128]{1,0:T(8,128)(2,1)S(1)}, bf16[872,128]{1,0:T(8,128)(2,1)S(1)}, u32[]{:S(2)}, u32[]{:S(2)}) collective-permute-start(bf16[872,128]{1,0:T(8,128)(2,1)S(1)} %shard_map.65), channel_id=1, source_target_pairs={{0,24},{4,28},{8,16},{12,20},{16,8},{20,12},{24,0},{28,4},{1,25},{... | collective-permute-start | bytes 669704 | tf_op jit(solution)/shard_map/ppermute | solution.py:245
  7.4 30.3 %collective-permute-start.1 = (bf16[872,128]{1,0:T(8,128)(2,1)S(1)}, bf16[872,128]{1,0:T(8,128)(2,1)S(1)}, u32[]{:S(2)}, u32[]{:S(2)}) collective-permute-start(bf16[872,128]{1,0:T(8,128)(2,1)S(1)} %get-tuple-element.15), channel_id=1, source_target_pairs={{0,16},{4,20},{8,24},{12,28},{16,0},{20,4},{24,8},{28,12},{1,17},{... | collective-permute-start | bytes 669704 | tf_op jit(solution)/shard_map/ppermute | solution.py:245
  7.4 35.4 %collective-permute-start.2 = (bf16[872,128]{1,0:T(8,128)(2,1)S(1)}, bf16[872,128]{1,0:T(8,128)(2,1)S(1)}, u32[]{:S(2)}, u32[]{:S(2)}) collective-permute-start(bf16[872,128]{1,0:T(8,128)(2,1)S(1)} %get-tuple-element.16), channel_id=1, source_target_pairs={{0,8},{4,12},{8,0},{12,4},{16,24},{20,28},{24,16},{28,20},{1,9},{5... | collective-permute-start | bytes 669704 | tf_op jit(solution)/shard_map/ppermute | solution.py:245
  8.0 17.2 %collective-permute-start.10 = (bf16[576,128]{1,0:T(8,128)(2,1)S(1)}, bf16[576,128]{1,0:T(8,128)(2,1)S(1)}, u32[]{:S(2)}, u32[]{:S(2)}) collective-permute-start(bf16[576,128]{1,0:T(8,128)(2,1)S(1)} %get-tuple-element.20), channel_id=1, source_target_pairs={{0,24},{4,28},{8,16},{12,20},{16,8},{20,12},{24,0},{28,4},{1,25},{... | collective-permute-start | bytes 442376 | tf_op jit(solution)/shard_map/ppermute | solution.py:245
  11.8 25.8 %collective-permute-start.11 = (bf16[576,128]{1,0:T(8,128)(2,1)S(1)}, bf16[576,128]{1,0:T(8,128)(2,1)S(1)}, u32[]{:S(2)}, u32[]{:S(2)}) collective-permute-start(bf16[576,128]{1,0:T(8,128)(2,1)S(1)} %get-tuple-element.21), channel_id=1, source_target_pairs={{0,16},{4,20},{8,24},{12,28},{16,0},{20,4},{24,8},{28,12},{1,17},{... | collective-permute-start | bytes 442376 | tf_op jit(solution)/shard_map/ppermute | solution.py:245
  11.8 0.7 %copy-start = (s32[768]{0:T(1024)S(1)}, s32[768]{0:T(1024)}, u32[]{:S(2)}) copy-start(s32[768]{0:T(1024)} %param.9) | copy-start | bytes 9220
  25.2 18.1 %collective-permute-start.3 = (bf16[872,128]{1,0:T(8,128)(2,1)S(1)}, bf16[872,128]{1,0:T(8,128)(2,1)S(1)}, u32[]{:S(2)}, u32[]{:S(2)}) collective-permute-start(bf16[872,128]{1,0:T(8,128)(2,1)S(1)} %get-tuple-element.14.refs_0_), channel_id=1, source_target_pairs={{0,4},{4,0},{8,12},{12,8},{16,20},{20,16},{24,28},{28,24},{1,5},{5... | collective-permute-start | bytes 669704 | tf_op jit(solution)/shard_map/ppermute | solution.py:248
  37.7 5.1 %collective-permute-start.12 = (bf16[576,128]{1,0:T(8,128)(2,1)S(1)}, bf16[576,128]{1,0:T(8,128)(2,1)S(1)}, u32[]{:S(2)}, u32[]{:S(2)}) collective-permute-start(bf16[576,128]{1,0:T(8,128)(2,1)S(1)} %get-tuple-element.22), channel_id=1, source_target_pairs={{0,8},{4,12},{8,0},{12,4},{16,24},{20,28},{24,16},{28,20},{1,9},{5... | collective-permute-start | bytes 442376 | tf_op jit(solution)/shard_map/ppermute | solution.py:245
  37.7 5.7 %collective-permute-start.4 = (bf16[872,128]{1,0:T(8,128)(2,1)S(1)}, bf16[872,128]{1,0:T(8,128)(2,1)S(1)}, u32[]{:S(2)}, u32[]{:S(2)}) collective-permute-start(bf16[872,128]{1,0:T(8,128)(2,1)S(1)} %collective-permute-done.refs_1_), channel_id=1, source_target_pairs={{0,4},{4,0},{8,12},{12,8},{16,20},{20,16},{24,28},{28,24},{1,5},{5... | collective-permute-start | bytes 669704 | tf_op jit(solution)/shard_map/ppermute | solution.py:248
  37.7 6.2 %collective-permute-start.5 = (bf16[872,128]{1,0:T(8,128)(2,1)S(1)}, bf16[872,128]{1,0:T(8,128)(2,1)S(1)}, u32[]{:S(2)}, u32[]{:S(2)}) collective-permute-start(bf16[872,128]{1,0:T(8,128)(2,1)S(1)} %collective-permute-done.1.refs_2_), channel_id=1, source_target_pairs={{0,4},{4,0},{8,12},{12,8},{16,20},{20,16},{24,28},{28,24},{1,5},{5... | collective-permute-start | bytes 669704 | tf_op jit(solution)/shard_map/ppermute | solution.py:248
  42.8 7.8 %collective-permute-start.13 = (bf16[576,128]{1,0:T(8,128)(2,1)S(1)}, bf16[576,128]{1,0:T(8,128)(2,1)S(1)}, u32[]{:S(2)}, u32[]{:S(2)}) collective-permute-start(bf16[576,128]{1,0:T(8,128)(2,1)S(1)} %get-tuple-element.19.refs_0_), channel_id=1, source_target_pairs={{0,4},{4,0},{8,12},{12,8},{16,20},{20,16},{24,28},{28,24},{1,5},{5... | collective-permute-start | bytes 442376 | tf_op jit(solution)/shard_map/ppermute | solution.py:248
  42.8 7.9 %collective-permute-start.14 = (bf16[576,128]{1,0:T(8,128)(2,1)S(1)}, bf16[576,128]{1,0:T(8,128)(2,1)S(1)}, u32[]{:S(2)}, u32[]{:S(2)}) collective-permute-start(bf16[576,128]{1,0:T(8,128)(2,1)S(1)} %collective-permute-done.10.refs_1_), channel_id=1, source_target_pairs={{0,4},{4,0},{8,12},{12,8},{16,20},{20,16},{24,28},{28,24},{1,5},{5... | collective-permute-start | bytes 442376 | tf_op jit(solution)/shard_map/ppermute | solution.py:248
  43.3 9.3 %collective-permute-start.15 = (bf16[576,128]{1,0:T(8,128)(2,1)S(1)}, bf16[576,128]{1,0:T(8,128)(2,1)S(1)}, u32[]{:S(2)}, u32[]{:S(2)}) collective-permute-start(bf16[576,128]{1,0:T(8,128)(2,1)S(1)} %collective-permute-done.11.refs_2_), channel_id=1, source_target_pairs={{0,4},{4,0},{8,12},{12,8},{16,20},{20,16},{24,28},{28,24},{1,5},{5... | collective-permute-start | bytes 442376 | tf_op jit(solution)/shard_map/ppermute | solution.py:248
  43.4 9.2 %collective-permute-start.16 = (bf16[576,128]{1,0:T(8,128)(2,1)S(1)}, bf16[576,128]{1,0:T(8,128)(2,1)S(1)}, u32[]{:S(2)}, u32[]{:S(2)}) collective-permute-start(bf16[576,128]{1,0:T(8,128)(2,1)S(1)} %collective-permute-done.12.refs_3_), channel_id=1, source_target_pairs={{0,4},{4,0},{8,12},{12,8},{16,20},{20,16},{24,28},{28,24},{1,5},{5... | collective-permute-start | bytes 442376 | tf_op jit(solution)/shard_map/ppermute | solution.py:248
  43.8 1.5 %collective-permute-start.6 = (bf16[872,128]{1,0:T(8,128)(2,1)S(1)}, bf16[872,128]{1,0:T(8,128)(2,1)S(1)}, u32[]{:S(2)}, u32[]{:S(2)}) collective-permute-start(bf16[872,128]{1,0:T(8,128)(2,1)S(1)} %collective-permute-done.2.refs_3_), channel_id=1, source_target_pairs={{0,4},{4,0},{8,12},{12,8},{16,20},{20,16},{24,28},{28,24},{1,5},{5... | collective-permute-start | bytes 669704 | tf_op jit(solution)/shard_map/ppermute | solution.py:248
  46.4 10.9 %collective-permute-start.7 = (bf16[3,96,128]{2,1,0:T(8,128)(2,1)S(1)}, bf16[3,96,128]{2,1,0:T(8,128)(2,1)S(1)}, u32[]{:S(2)}, u32[]{:S(2)}) collective-permute-start(bf16[3,96,128]{2,1,0:T(8,128)(2,1)S(1)} %shard_map.67), channel_id=1, source_target_pairs={{0,24},{4,28},{8,16},{12,20},{16,8},{20,12},{24,0},{28,4},{1,25},{... | collective-permute-start | bytes 221192 | tf_op jit(solution)/shard_map/ppermute | solution.py:245
  50.6 10.2 %collective-permute-start.8 = (bf16[3,96,128]{2,1,0:T(8,128)(2,1)S(1)}, bf16[3,96,128]{2,1,0:T(8,128)(2,1)S(1)}, u32[]{:S(2)}, u32[]{:S(2)}) collective-permute-start(bf16[3,96,128]{2,1,0:T(8,128)(2,1)S(1)} %shard_map.68), channel_id=1, source_target_pairs={{0,16},{4,20},{8,24},{12,28},{16,0},{20,4},{24,8},{28,12},{1,17},{... | collective-permute-start | bytes 221192 | tf_op jit(solution)/shard_map/ppermute | solution.py:245
  50.7 10.2 %collective-permute-start.9 = (bf16[3,96,128]{2,1,0:T(8,128)(2,1)S(1)}, bf16[3,96,128]{2,1,0:T(8,128)(2,1)S(1)}, u32[]{:S(2)}, u32[]{:S(2)}) collective-permute-start(bf16[3,96,128]{2,1,0:T(8,128)(2,1)S(1)} %shard_map.69), channel_id=1, source_target_pairs={{0,8},{4,12},{8,0},{12,4},{16,24},{20,28},{24,16},{28,20},{1,9},{5... | collective-permute-start | bytes 221192 | tf_op jit(solution)/shard_map/ppermute | solution.py:245
  53.3 8.3 %collective-permute-start.17 = (bf16[2,96,128]{2,1,0:T(8,128)(2,1)S(1)}, bf16[2,96,128]{2,1,0:T(8,128)(2,1)S(1)}, u32[]{:S(2)}, u32[]{:S(2)}) collective-permute-start(bf16[2,96,128]{2,1,0:T(8,128)(2,1)S(1)} %shard_map.72), channel_id=1, source_target_pairs={{0,24},{4,28},{8,16},{12,20},{16,8},{20,12},{24,0},{28,4},{1,25},{... | collective-permute-start | bytes 147464 | tf_op jit(solution)/shard_map/ppermute | solution.py:245
  56.6 5.2 %collective-permute-start.18 = (bf16[2,96,128]{2,1,0:T(8,128)(2,1)S(1)}, bf16[2,96,128]{2,1,0:T(8,128)(2,1)S(1)}, u32[]{:S(2)}, u32[]{:S(2)}) collective-permute-start(bf16[2,96,128]{2,1,0:T(8,128)(2,1)S(1)} %shard_map.73), channel_id=1, source_target_pairs={{0,16},{4,20},{8,24},{12,28},{16,0},{20,4},{24,8},{28,12},{1,17},{... | collective-permute-start | bytes 147464 | tf_op jit(solution)/shard_map/ppermute | solution.py:245
  57.4 4.7 %collective-permute-start.19 = (bf16[2,96,128]{2,1,0:T(8,128)(2,1)S(1)}, bf16[2,96,128]{2,1,0:T(8,128)(2,1)S(1)}, u32[]{:S(2)}, u32[]{:S(2)}) collective-permute-start(bf16[2,96,128]{2,1,0:T(8,128)(2,1)S(1)} %shard_map.74), channel_id=1, source_target_pairs={{0,8},{4,12},{8,0},{12,4},{16,24},{20,28},{24,16},{28,20},{1,9},{5... | collective-permute-start | bytes 147464 | tf_op jit(solution)/shard_map/ppermute | solution.py:245
